TPU v7x, 128 devices: a whole 4x4x4 slice. The times are simulated.
128 devices in a mesh: seq: 32 (over y, x, core), head: 4 (over z).
Axes of the slice: x: 4, y: 4, z: 4, core: 2. Of those that a mesh axis runs over, the one named last changes fastest.
Arguments:
- byte_in: bfloat16 [4096, 8, 1024], P('seq'), may hold values from -6 to 6
- local_gain: float32 [1024], replicated, may hold values from 0.25 to 1.75
- local_qkv: bfloat16 [1024, 3, 1024], P(None, None, 'head'), may hold values from -0.1875 to 0.1875
- local_out: bfloat16 [1024, 1024], P('head'), may hold values from -0.1875 to 0.1875
- mlp_up: bfloat16 [1024, 4096], P(None, 'head'), may hold values from -0.1875 to 0.1875
- mlp_down: bfloat16 [4096, 1024], P('head'), may hold values from -0.09375 to 0.09375
- local_scale: float32 [8], P('head'), may hold values from 1 to 40
- patch_proj: bfloat16 [1024, 256], replicated, may hold values from -0.1875 to 0.1875
- global_gain: float32 [2048], replicated, may hold values from 0.25 to 1.75
- global_qkv: bfloat16 [2048, 3, 2048], P(None, None, 'head'), may hold values from -0.125 to 0.125
- global_out: bfloat16 [2048, 2048], P('head'), may hold values from -0.125 to 0.125
- global_scale: float32 [16], P('head'), may hold values from 1 to 40
- back_proj: bfloat16 [256, 1024], replicated, may hold values from -0.375 to 0.375
- owners: int32 [32, 64], replicated, may hold values from 0 to 31, as said below
Outputs:
- byte_out: bfloat16 [4096, 8, 1024], P('seq', 'head')
- global_state: bfloat16 [4096, 2048], P('seq', 'head')
Inputs may be any that keep to these rules, and one draw needn't show every extreme that they name: `owners`: row s names, for each of the 64 blocks of 2 patches of byte range s in order, its owner; each row names every owner exactly twice.
All inputs are finite; a program needn't handle non-finite values.
Results may differ from a plain program's by a relative error of at most 0.028.
The roundings to bfloat16 on the way count: a program that leaves them out, or rounds other values in their place, can miss the bound.
Values may be sent and summed in bfloat16 or wider, within the bound.
A program may use at most 128 MiB of HBM per device.

v0:
```python
import math

import jax
import jax.numpy as jnp
from jax import lax
from jax.sharding import PartitionSpec as P

EPSILON = 1e-06
NEGATIVE = -1e30


def sent_together(arrays, axis, dim, along):
    both = jnp.concatenate(arrays, axis=along)
    whole, at, outs = (lax.all_gather(both, axis, axis=dim, tiled=True), 0, [])
    for a in arrays:
        outs.append(lax.slice_in_dim(whole, at, at + a.shape[along], axis=along))
        at += a.shape[along]
    return tuple(outs)


def split_up(x, dim, peers):
    lengths = x.shape
    pieces = x.reshape(*lengths[:dim], peers, lengths[dim] // peers, *lengths[dim + 1 :])
    return jnp.moveaxis(pieces, dim, 0)


def sent_and_summed(x, axis, dim):
    peers = lax.axis_size(axis)
    pieces = lax.all_to_all(split_up(x, dim, peers), axis, 0, 0, tiled=True)
    return jnp.sum(pieces.astype(jnp.float32), axis=0)


def rms_norm(values, gain):
    mean_square = jnp.mean(values * values, axis=-1, keepdims=True)
    return values * lax.rsqrt(mean_square + EPSILON) * gain


def unit_heads(values, head_count):
    shaped = values.reshape(values.shape[0], head_count, -1)
    mean_square = jnp.mean(shaped * shaped, axis=-1, keepdims=True)
    return shaped * lax.rsqrt(mean_square + EPSILON)


def patch_attention(queries, key_rows, values, head_scale):
    patch_span = queries.shape[1]
    head_depth = queries.shape[-1]
    scores = jnp.einsum("pihd,pjhd->phij", queries, key_rows, preferred_element_type=jnp.float32)
    scores = scores * (head_scale[:, None, None] / math.sqrt(head_depth))
    causal = jnp.tril(jnp.ones((patch_span, patch_span), dtype=bool))
    scores = jnp.where(causal, scores, NEGATIVE)
    row_max = jnp.max(scores, axis=-1, keepdims=True)
    weights = jnp.where(causal, jnp.exp(scores - row_max), 0.0)
    weight_sum = jnp.sum(weights, axis=-1)
    summed = jnp.einsum(
        "phij,pjhd->pihd", weights.astype(jnp.bfloat16), values, preferred_element_type=jnp.float32
    )
    return (summed / jnp.transpose(weight_sum, (0, 2, 1))[..., None]).astype(jnp.bfloat16)


def route_plan(owners, source):
    listed = lax.dynamic_index_in_dim(owners, source, 0, keepdims=False)
    block_count = listed.shape[0]
    indices = jnp.arange(block_count, dtype=jnp.int32)
    earlier = (listed[None, :] == listed[:, None]) & (indices[None, :] < indices[:, None])
    rank_of = jnp.sum(earlier, axis=1)
    per_owner = block_count // owners.shape[0]
    slot_of = listed * per_owner + rank_of
    inverse = jnp.sum(jnp.where(slot_of[None, :] == indices[:, None], indices[None, :], 0), axis=1)
    return (slot_of, inverse)


def reorder_blocks(row_data, chosen_blocks):
    blocks = row_data.reshape(chosen_blocks.shape[0], -1, row_data.shape[-1])
    return jnp.take(blocks, chosen_blocks, axis=0).reshape(row_data.shape)


def attend_piece(carried, key_piece, queries, query_pos, key_table, head_scale):
    key_rows, value_rows = key_piece
    row_count = key_rows.shape[0]
    head_count = queries.shape[1]
    head_depth = queries.shape[2]

    def compute(running):
        running_max, running_sum, accumulated = running
        keys_three = key_rows.reshape(row_count, head_count, head_depth)
        values_three = value_rows.reshape(row_count, head_count, head_depth)
        scores = jnp.einsum("qhd,khd->qhk", queries, keys_three, preferred_element_type=jnp.float32)
        scores = scores * (head_scale[None, :, None] / math.sqrt(head_depth))
        visible = key_table[None, None, :] <= query_pos[:, None, None]
        scores = jnp.where(visible, scores, NEGATIVE)
        new_max = jnp.maximum(running_max, jnp.max(scores, axis=-1))
        weights = jnp.where(visible, jnp.exp(scores - new_max[..., None]), 0.0)
        new_sum = jnp.sum(weights, axis=-1)
        summed = jnp.einsum(
            "qhk,khd->qhd",
            weights.astype(jnp.bfloat16),
            values_three,
            preferred_element_type=jnp.float32,
        )
        return (new_max, new_sum, summed)

    def keep(running):
        return running

    return lax.cond(jnp.min(key_table) > jnp.max(query_pos), keep, compute, carried)


def on_device(
    byte_in,
    local_gain,
    local_qkv,
    local_out,
    mlp_up,
    mlp_down,
    local_scale,
    patch_proj,
    global_gain,
    global_qkv,
    global_out,
    global_scale,
    back_proj,
    owners,
):
    patches, patch_span, model_width = byte_in.shape
    head_index = lax.axis_index("head")
    own_count = patch_span // lax.axis_size("head")
    byte_rows = byte_in.reshape(-1, model_width).astype(jnp.float32)
    normed = rms_norm(byte_rows, local_gain).astype(jnp.bfloat16)
    head_part = local_qkv.shape[2]
    local_heads = local_scale.shape[0]
    projected = jnp.dot(
        normed, local_qkv.reshape(model_width, 3 * head_part), preferred_element_type=jnp.float32
    )
    queries = (
        unit_heads(projected[:, :head_part], local_heads)
        .astype(jnp.bfloat16)
        .reshape(patches, patch_span, local_heads, -1)
    )
    key_rows = (
        unit_heads(projected[:, head_part : 2 * head_part], local_heads)
        .astype(jnp.bfloat16)
        .reshape(patches, patch_span, local_heads, -1)
    )
    values = (
        projected[:, 2 * head_part :]
        .astype(jnp.bfloat16)
        .reshape(patches, patch_span, local_heads, -1)
    )
    attended = patch_attention(queries, key_rows, values, local_scale).reshape(-1, head_part)
    activated = jax.nn.gelu(
        jnp.dot(normed, mlp_up, preferred_element_type=jnp.float32), approximate=True
    ).astype(jnp.bfloat16)
    partial_sum = jnp.dot(attended, local_out, preferred_element_type=jnp.float32) + jnp.dot(
        activated, mlp_down, preferred_element_type=jnp.float32
    )
    shares = lax.psum_scatter(
        partial_sum.reshape(patches, patch_span, model_width),
        "head",
        scatter_dimension=1,
        tiled=True,
    )
    own_input = lax.dynamic_slice_in_dim(byte_in, head_index * own_count, own_count, 1).astype(
        jnp.float32
    )
    own_state = (own_input + shares).astype(jnp.bfloat16)
    own_patch = (
        jnp.dot(own_state.reshape(-1, model_width), patch_proj, preferred_element_type=jnp.float32)
        .reshape(patches, -1)
        .astype(jnp.bfloat16)
    )
    patch_in = lax.all_gather(own_patch, "head", axis=1, tiled=True)
    head_width = global_qkv.shape[2]
    head_group = global_scale.shape[0]
    gnormed = rms_norm(patch_in.astype(jnp.float32), global_gain).astype(jnp.bfloat16)
    global_mixed = jnp.dot(
        gnormed, global_qkv.reshape(-1, 3 * head_width), preferred_element_type=jnp.float32
    )
    global_query = (
        unit_heads(global_mixed[:, :head_width], head_group)
        .astype(jnp.bfloat16)
        .reshape(patches, head_width)
    )
    global_keys = (
        unit_heads(global_mixed[:, head_width : 2 * head_width], head_group)
        .astype(jnp.bfloat16)
        .reshape(patches, head_width)
    )
    global_values = global_mixed[:, 2 * head_width :].astype(jnp.bfloat16)
    residual = lax.dynamic_slice_in_dim(patch_in, head_index * head_width, head_width, 1)
    seq_index = lax.axis_index("seq")
    seq_count = lax.axis_size("seq")
    slot_of, inverse = route_plan(owners, seq_index)
    routed_query, routed_keys, routed_values, routed_residual = (
        global_query,
        global_keys,
        global_values,
        residual,
    )
    key_table = jnp.arange(patches * seq_count, dtype=jnp.int32)
    query_pos = lax.dynamic_slice_in_dim(key_table, seq_index * patches, patches)
    query_three = routed_query.reshape(patches, head_group, -1)
    head_depth = query_three.shape[-1]
    start_state = (
        jnp.full((patches, head_group), NEGATIVE, jnp.float32),
        jnp.zeros((patches, head_group), jnp.float32),
        jnp.zeros((patches, head_group, head_depth), jnp.float32),
    )
    final_max, final_sum, accumulated = attend_piece(
        start_state,
        sent_together((routed_keys, routed_values), "seq", 0, 1),
        query_three,
        query_pos,
        key_table,
        global_scale,
    )
    global_attended = (accumulated / final_sum[..., None]).astype(jnp.bfloat16).reshape(patches, -1)
    update = sent_and_summed(
        jnp.dot(global_attended, global_out, preferred_element_type=jnp.float32).astype(
            jnp.bfloat16
        ),
        "head",
        1,
    )
    result = (update + routed_residual.astype(jnp.float32)).astype(jnp.bfloat16)
    global_state = lax.all_to_all(
        reorder_blocks(result, inverse), "seq", split_axis=0, concat_axis=0, tiled=True
    )
    back_term = jnp.dot(
        result.reshape(-1, back_proj.shape[0]), back_proj, preferred_element_type=jnp.float32
    )
    byte_out = (
        (own_state.reshape(-1, model_width).astype(jnp.float32) + back_term)
        .reshape(patches, own_count, model_width)
        .astype(jnp.bfloat16)
    )
    return (byte_out, global_state)


def solution(mesh):
    placed = (
        P("seq", None, None),
        P(),
        P(None, None, "head"),
        P("head", None),
        P(None, "head"),
        P("head", None),
        P("head"),
        P(),
        P(),
        P(None, None, "head"),
        P("head", None),
        P("head"),
        P(),
        P(),
    )
    return jax.shard_map(
        on_device,
        mesh=mesh,
        in_specs=placed,
        out_specs=(P("seq", "head", None), P("seq", "head")),
        check_vma=False,
    )
```

profile of v0, /device:TPU:1, one launch (start us, length us, event | category | flops | bytes accessed | tf_op | source)
XLA Modules:
  0.0 246.9 jit_solution(9578977157080254354)
XLA Ops:
  7.2 2.2 fusion.12
  9.5 2.6 %copy.115 = bf16[1024,3,256]{0,2,1:T(8,128)(2,1)} copy(bf16[1024,3,256]{2,0,1:T(8,128)(2,1)} %param.18) | data formatting | bytes 3145728 | tf_op args[2]
  12.1 3.9 %fusion.31 = f32[1024,768]{0,1:T(8,128)S(1)} fusion(bf16[1024,768]{0,1:T(8,128)(2,1)} %bitcast.127, bf16[128,8,1024]{2,1,0:T(8,128)(2,1)} %param.16, f32[1024]{0:T(1024)S(1)} %copy-done.5, f32[128,8]{1,0:T(8,128)S(1)} %add_rsqrt_fusion.1), kind=kOutput, calls=%fused_computation.38 | convolution fusion | flops 1614807040 | bytes 6823936 | tf_op jit(solution)/shard_map/dot_general | solution.py:131
  16.0 0.2 bitcast_reduce_fusion.1
  16.3 1.2 fusion.86
  17.4 0.9 slice.51
  18.4 0.1 rsqrt.60
  18.5 0.1 copy.118
  18.6 0.1 rsqrt.62
  18.9 2.6 %copy.117 = f32[1024,256]{1,0:T(8,128)} copy(f32[1024,256]{0,1:T(8,128)} %get-tuple-element.59) | data formatting | bytes 2097152 | tf_op jit(solution)/shard_map/slice | solution.py:135
  21.4 1.4 copy.119
  22.8 2.3 fusion.57
  25.0 0.4 copy.121
  25.5 0.1 fusion.88
  25.6 0.4 copy.122
  26.0 0.1 copy.123
  26.2 1.2 copy.116
  27.5 8.8 %fusion.26 = f32[1024,1024]{1,0:T(8,128)} fusion(bf16[1024,1024]{1,0:T(8,128)(2,1)S(1)} %copy-done, bf16[1024,1024]{1,0:T(8,128)(2,1)} %param.20, bf16[128,8,1024]{2,1,0:T(8,128)(2,1)} %param.16, f32[1024]{0:T(1024)S(1)} %copy-done.5, f32[1024]{0:T(1024)S(1)} %rsqrt.63), kind=kOutput, calls=%fused_computation.35 | convolution fusion | flops 4308598784 | bytes 10493952 | tf_op jit(solution)/shard_map/dot_general | solution.py:153
  36.3 5.4 %add_bitcast_fusion = f32[128,8,1024]{2,1,0:T(8,128)} fusion(f32[1024,1024]{1,0:T(8,128)} %fusion.26, bf16[256,1024]{1,0:T(8,128)(2,1)} %param.19, bf16[128,2,8,8]{3,2,1,0:T(8,128)(2,1)S(1)} %copy.122, bf16[1024,256]{1,0:T(8,128)(2,1)S(1)} %copy.116, f32[128,8,2]{1,2,0:T(2,128)S(1)} %copy.123), kind=kOutput, calls=%fused_computation.33 | convolution fusion | flops 542638080 | bytes 9478144 | tf_op jit(solution)/shard_map/dot_general | solution.py:153
  41.6 6.8 %copy.124 = f32[128,8,1024]{2,0,1:T(8,128)} copy(f32[128,8,1024]{2,1,0:T(8,128)} %add_bitcast_fusion) | data formatting | bytes 8388608 | tf_op jit(solution)/shard_map/reshape | solution.py:157
  48.5 8.8 %copy.126 = bf16[2048,3,512]{0,2,1:T(8,128)(2,1)} copy(bf16[2048,3,512]{2,0,1:T(8,128)(2,1)} %param.25) | data formatting | bytes 12582912 | tf_op args[9]
  57.4 2.2 constant_dynamic-slice_fusion.1
  59.6 39.3 %reduce-scatter.2.cloned.1.call-done = f32[128,2,1024]{2,0,1:T(8,128)} async-done(((f32[128,8,1024]{2,0,1:T(8,128)}), f32[128,2,1024]{2,0,1:T(8,128)}) %reduce-scatter.2.cloned.1.call-update) | async-done | bytes 1048592 | tf_op jit(solution)/shard_map/reduce_scatter | solution.py:156
  98.8 1.4 add_convert_fusion
  100.2 0.5 copy.125
  100.8 0.2 reshape.233
  101.0 0.3 convolution_convert_fusion.1
  101.4 9.9 %all_gather.6 = bf16[128,2048]{1,0:T(8,128)(2,1)S(1)} all-gather(bf16[128,512]{1,0:T(8,128)(2,1)S(1)} %convert_element_type.111), channel_id=1, replica_groups=mesh['seq'=32,'head'=4] {'head'}, dimensions={1}, use_global_device_ids=true | all-gather | bytes 655360 | tf_op jit(solution)/shard_map/all_gather | solution.py:171
  111.3 0.2 fusion.52
  111.5 5.0 %fusion.60 = f32[128,1536]{1,0:T(8,128)S(1)} fusion(bf16[2048,1536]{0,1:T(8,128)(2,1)} %bitcast.122, bf16[128,2048]{1,0:T(8,128)(2,1)S(1)} %all_gather.6, f32[2048]{0:T(1024)S(1)} %copy-done.4, f32[128]{0:T(128)S(1)} %add_rsqrt_fusion.5), kind=kOutput, calls=%fused_computation.72 | convolution fusion | flops 806354944 | bytes 7610880 | tf_op jit(solution)/shard_map/dot_general | solution.py:175
  116.6 0.2 reduce_sum.110
  116.9 0.2 mul.198
  117.2 0.7 pad_maximum_fusion
  117.9 0.6 fusion.84
  119.2 0.7 fusion.78
  119.9 0.2 convert_reduce_fusion.1
  120.1 0.7 fusion.77
  120.8 0.1 select_reduce_fusion
  120.9 0.1 reduce_sum.116
  121.1 0.2 multiply_reduce_fusion
  121.4 0.2 fusion.70
  121.6 52.8 %all-gather.2.cloned.1.call-done = bf16[4096,1024]{1,0:T(8,128)(2,1)} async-done(((bf16[128,1024]{1,0:T(8,128)(2,1)}), bf16[4096,1024]{1,0:T(8,128)(2,1)}) %all-gather.2.cloned.1.call-update) | async-done | bytes 8388624 | tf_op jit(solution)/shard_map/all_gather | solution.py:14
  174.3 31.4 %conditional.1 = (f32[128,4]{0,1:T(4,128)S(1)}, f32[128,4,128]{0,2,1:T(8,128)S(1)}) conditional(s32[]{:T(128)} %convert_element_type.109, (s32[4096]{0:T(1024)S(1)}, s32[128]{0:T(128)S(1)}, bf16[4096,1024]{1,0:T(8,128)(2,1)}, bf16[128,4,128]{2,0,1:T(8,128)(2,1)S(1)}, f32[4]{0:T(128)S(1)}) %tuple.42, () %tuple.17), branch_computations={%region_10.13_spmd, %region_13.14_spmd} | conditional | flops 1101528576 | bytes 103707256 | solution.py:105
  174.3 1.8 broadcast_compare_fusion
  176.2 11.5 %copy.131 = bf16[4096,1024]{0,1:T(8,128)(2,1)} copy(bf16[4096,1024]{1,0:T(8,128)(2,1)} %get-tuple-element.48) | data formatting | bytes 16777216 | tf_op jit(solution)/shard_map
  187.7 3.9 %fusion.85 = (bf16[4096,512]{0,1:T(8,128)(2,1)S(1)}, bf16[4096,512]{0,1:T(8,128)(2,1)S(1)}) fusion(bf16[4096,1024]{0,1:T(8,128)(2,1)} %copy.131), kind=kLoop, calls=%fused_computation.127 | loop fusion | bytes 16777216 | tf_op jit(solution)/shard_map/slice | solution.py:16
  191.6 2.7 %fusion = (f32[128,4]{0,1:T(4,128)S(1)}, f32[4,4096,128]{2,1,0:T(8,128)S(1)}) fusion(f32[4]{0:T(128)S(1)} %broadcast_multiply_fusion, pred[128,4096]{0,1:T(8,128)(4,1)S(1)} %broadcast_compare_fusion, bf16[4096,4,128]{0,2,1:T(8,128)(2,1)S(1)} %bitcast.123, bf16[128,4,128]{2,0,1:T(8,128)(2,1)S(1)} %get-tuple-element.16), kind=kOutput, calls=%fused_computation.3 | convolution fusion | flops 543161856 | bytes 13240336 | tf_op jit(solution)/shard_map/cond/branch_0_fun/qhd,khd->qhk/dot_general | solution.py:87
  194.3 3.2 %copy-done.2 = f32[4,4096,128]{2,1,0:T(8,128)} copy-done((f32[4,4096,128]{2,1,0:T(8,128)}, f32[4,4096,128]{2,1,0:T(8,128)S(1)}, u32[]{:S(2)}) %copy-start.2) | copy-done | bytes 8388632 | tf_op jit(solution)/shard_map/cond
  197.5 3.3 %fusion.6 = f32[128,4,128]{2,0,1:T(8,128)S(1)} fusion(bf16[4096,4,128]{0,2,1:T(8,128)(2,1)S(1)} %bitcast.124, f32[4,4096,128]{2,1,0:T(8,128)S(1)} %get-tuple-element.57, f32[128,4]{0,1:T(4,128)S(1)} %broadcast_maximum_fusion, f32[4]{0:T(128)S(1)} %broadcast_multiply_fusion, pred[128,4096]{0,1:T(8,128)(4,1)S(1)} %broadcast_compare_fusion), kind=kOutput, calls=%fused_computation.8 | convolution fusion | flops 547356672 | bytes 13371408 | tf_op jit(solution)/shard_map/cond/branch_0_fun/qhk,khd->qhd/dot_general | solution.py:94
  200.8 0.1 copy.139
  200.9 4.6 %fusion.2 = f32[128,4]{0,1:T(4,128)S(1)} fusion(f32[4,4096,128]{2,1,0:T(8,128)} %copy-done.2, f32[128,4]{0,1:T(4,128)S(1)} %broadcast_maximum_fusion, f32[4]{0:T(128)S(1)} %broadcast_multiply_fusion, pred[128,4096]{0,1:T(8,128)(4,1)S(1)} %broadcast_compare_fusion), kind=kLoop, calls=%fused_computation.5 | loop fusion | flops 10485248 | bytes 8917008 | tf_op jit(solution)/shard_map/cond/branch_0_fun/reduce_sum | solution.py:93
  205.8 2.2 convolution_convert_fusion
  208.0 0.8 copy.150
  208.9 4.1 %all-to-all-start = ((bf16[4,128,512]{2,1,0:T(8,128)(2,1)}), bf16[4,128,512]{2,1,0:T(8,128)(2,1)}, u32[]{:S(2)}, u32[]{:S(2)}) async-start(bf16[4,128,512]{2,1,0:T(8,128)(2,1)} %bitcast.125), calls=%async_computation.1 | async-start | bytes 1048576 | tf_op jit(solution)/shard_map/all_to_all | solution.py:29
  213.1 0.1 copy.135
  213.3 8.9 %all-to-all-done = bf16[4,128,512]{2,1,0:T(8,128)(2,1)} async-done(((bf16[4,128,512]{2,1,0:T(8,128)(2,1)}), bf16[4,128,512]{2,1,0:T(8,128)(2,1)}, u32[]{:S(2)}, u32[]{:S(2)}) %all-to-all-start) | async-done | bytes 524320 | tf_op jit(solution)/shard_map/all_to_all | solution.py:29
  222.1 1.1 convert_reduce_fusion
  223.5 0.8 gather_fusion
  224.4 0.8 broadcast_select_fusion
  225.1 6.6 %all-to-all-start.1 = ((bf16[32,4,512]{2,1,0:T(4,128)(2,1)}), bf16[32,4,512]{2,1,0:T(4,128)(2,1)S(1)}, u32[]{:S(2)}, u32[]{:S(2)}) async-start(bf16[32,4,512]{2,1,0:T(4,128)(2,1)} %broadcast_select_fusion), calls=%async_computation.2 | async-start | bytes 262144 | tf_op jit(solution)/shard_map/all_to_all | solution.py:225
  231.8 1.3 fusion.43
  233.1 1.0 convert_element_type.122
  234.1 5.3 %all-to-all-done.1 = bf16[32,4,512]{2,1,0:T(4,128)(2,1)S(1)} async-done(((bf16[32,4,512]{2,1,0:T(4,128)(2,1)}), bf16[32,4,512]{2,1,0:T(4,128)(2,1)S(1)}, u32[]{:S(2)}, u32[]{:S(2)}) %all-to-all-start.1) | async-done | bytes 131104 | tf_op jit(solution)/shard_map/all_to_all | solution.py:225
  239.4 0.7 all_to_all.11
  (50 shorter events, 1.2 us)
Async XLA Ops:
  7.2 20.3 %copy-start = (bf16[1024,1024]{1,0:T(8,128)(2,1)S(1)}, bf16[1024,1024]{1,0:T(8,128)(2,1)}, u32[]{:S(2)}) copy-start(bf16[1024,1024]{1,0:T(8,128)(2,1)} %param.21) | copy-start | bytes 6291460
  7.2 4.9 %copy-start.5 = (f32[1024]{0:T(1024)S(1)}, f32[1024]{0:T(1024)}, u32[]{:S(2)}) copy-start(f32[1024]{0:T(1024)} %param.17) | copy-start | bytes 12292
  7.2 91.6 %reduce-scatter.2.cloned.1.call-start = ((), (), s32[]{:S(2)}) async-start(), calls=%async_computation.3 | async-start | bytes 5242880 | tf_op jit(solution)/shard_map/reduce_scatter | solution.py:156
  22.8 2.7 %copy-start.6 = (f32[2]{0:T(128)S(1)}, f32[2]{0:T(128)}, u32[]{:S(2)}) copy-start(f32[2]{0:T(128)} %param.22) | copy-start | bytes 28
  48.5 125.9 %all-gather.2.cloned.1.call-start = ((), (), s32[]{:S(2)}) async-start(), calls=%async_computation.4 | async-start | bytes 8650752 | tf_op jit(solution)/shard_map/all_gather | solution.py:14
  57.4 43.6 %copy-start.3 = (bf16[1024,256]{1,0:T(8,128)(2,1)S(1)}, bf16[1024,256]{1,0:T(8,128)(2,1)}, u32[]{:S(2)}) copy-start(bf16[1024,256]{1,0:T(8,128)(2,1)} %param.23) | copy-start | bytes 1572868
  57.4 54.1 %copy-start.4 = (f32[2048]{0:T(1024)S(1)}, f32[2048]{0:T(1024)}, u32[]{:S(2)}) copy-start(f32[2048]{0:T(1024)} %param.24) | copy-start | bytes 24580
  116.5 57.9 %copy-start.7 = (f32[4]{0:T(128)S(1)}, f32[4]{0:T(128)}, u32[]{:S(2)}) copy-start(f32[4]{0:T(128)} %param.27) | copy-start | bytes 52
  194.3 3.2 %copy-start.2 = (f32[4,4096,128]{2,1,0:T(8,128)}, f32[4,4096,128]{2,1,0:T(8,128)S(1)}, u32[]{:S(2)}) copy-start(f32[4,4096,128]{2,1,0:T(8,128)S(1)} %get-tuple-element.57) | copy-start | bytes 25165828 | tf_op jit(solution)/shard_map/cond
  205.8 34.3 %copy-start.1 = (bf16[1024,1024]{1,0:T(8,128)(2,1)S(1)}, bf16[1024,1024]{1,0:T(8,128)(2,1)}, u32[]{:S(2)}) copy-start(bf16[1024,1024]{1,0:T(8,128)(2,1)} %param.21) | copy-start | bytes 6291460
  208.9 13.3 %all-to-all-start = ((bf16[4,128,512]{2,1,0:T(8,128)(2,1)}), bf16[4,128,512]{2,1,0:T(8,128)(2,1)}, u32[]{:S(2)}, u32[]{:S(2)}) async-start(bf16[4,128,512]{2,1,0:T(8,128)(2,1)} %bitcast.125), calls=%async_computation.1 | async-start | bytes 1048576 | tf_op jit(solution)/shard_map/all_to_all | solution.py:29
  225.1 14.2 %all-to-all-start.1 = ((bf16[32,4,512]{2,1,0:T(4,128)(2,1)}), bf16[32,4,512]{2,1,0:T(4,128)(2,1)S(1)}, u32[]{:S(2)}, u32[]{:S(2)}) async-start(bf16[32,4,512]{2,1,0:T(4,128)(2,1)} %broadcast_select_fusion), calls=%async_computation.2 | async-start | bytes 262144 | tf_op jit(solution)/shard_map/all_to_all | solution.py:225
Sparse Core Ops, SparseCore 0:
  48.6 50.1 reduce-scatter.1
  118.0 56.2 all-gather.1
where the time goes:
time: 248 us; the launch traced here: 247 us
  waiting for transfers between devices  106 us (43%)
  local copies, waits for them, and re-layouts  53.7 us (22%)
  matrix products  35.2 us (14%)
  other arithmetic  15.7 us (6%)
  between operations  15.1 us (6%)
  starting transfers between devices  10.8 us (4%)
  blocking collectives  9.9 us (4%)
    all_gather x1, waiting for transfers between devices, sent_together(): whole, at, outs = (lax.all_gather(both, axis, axis=dim, tiled=True), 0, [])  52.8 us
    reduce_scatter x1, waiting for transfers between devices, on_device(): lax.psum_scatter(partial_sum.reshape(patches, patch_span, model_width), '...  39.3 us
    another operation x1, local copies, waits for them, and re-layouts  11.5 us
    unnamed x16, local copies, waits for them, and re-layouts  11.5 us
    all_gather x1, blocking collectives, on_device(): patch_in = lax.all_gather(own_patch, 'head', axis=1, tiled=True)  9.9 us
    all_to_all x1, waiting for transfers between devices, sent_and_summed(): pieces = lax.all_to_all(split_up(x, dim, peers), axis, 0, 0, tiled=True)  8.87 us
    dot_general x1, matrix products, on_device(): jnp.dot(activated, mlp_down, preferred_element_type=jnp.float32)  8.8 us
    reshape x1, local copies, waits for them, and re-layouts, on_device(): partial_sum.reshape(patches, patch_span, model_width)  6.83 us
  transfers between devices with their start and end apart: 4, of which 4 were waited for; matrix products, arithmetic and copies ran while one was open for 7% of the time, Pallas kernels for 0%

commit v1 on v0

v1 whole, which is shorter than its diff:
```python
import functools
import math

import jax
import jax.numpy as jnp
from jax import lax
from jax.experimental import pallas as pl
from jax.experimental.pallas import tpu as pltpu
from jax.sharding import PartitionSpec as P

EPS = 1e-06
NEG = -1e30
MESH = pl.DeviceIdType.MESH
F32 = jnp.float32
BF16 = jnp.bfloat16
XN = 4
YN = 4
ZN = 4
CHUNKS = 4
EARLY = 2
HD = 128


def dot(a, b):
    return jnp.dot(a, b, preferred_element_type=F32)


def dot_t(a, b):
    return lax.dot_general(a, b, (((1,), (1,)), ((), ())), preferred_element_type=F32)


def unit(v):
    return v * lax.rsqrt(jnp.mean(v * v, axis=-1, keepdims=True) + EPS)


def kernel(
    x_hbm, wqkv_hbm, wo_hbm, up_hbm, down_hbm, pp_hbm, gqkv_hbm, gout_hbm, back_hbm,
    gain_ref, ggain_ref, owners_ref, lscale_ref, gscale_ref,
    byte_ref, perm_ref,
    xv, wqkv, wo, up, down, ppw, gqkv, gout, back,
    act, part, ppf, bsend, brecv, ownf, ppsend, pprecv, ppown, pin,
    gn, qkvs, kvbuf, qbuf, m_ref, l_ref, acc, osend, orecv, rsend, rrecv, bst,
    lsem, pp_s, pp_r, ag_s, ag_r, bk_s, bk_r, xk_s, xk_r, xq_s, xq_r,
    y_s, y_r, c_s, c_r, o_s, o_r, r_s, r_r,
):
    s = lax.axis_index("seq")
    z = lax.axis_index("head")
    core = lax.rem(s, 2)
    x = lax.rem(s // 2, XN)
    y = s // (2 * XN)
    rows = xv.shape[0] // CHUNKS
    span = rows // 8
    own = 2 * span

    def seq_of(yy, xx, cc):
        return (yy * XN + xx) * 2 + cc

    def zpeer(d):
        return (s, lax.rem(z + d, ZN))

    def xpeer(d):
        return (seq_of(y, lax.rem(x + d, XN), core), z)

    y_up = (seq_of(lax.rem(y + 1, YN), x, core), z)
    y_down = (seq_of(lax.rem(y + YN - 1, YN), x, core), z)
    sibling = (seq_of(y, x, 1 - core), z)

    loads = [
        pltpu.make_async_copy(a, b, lsem.at[i])
        for i, (a, b) in enumerate(
            ((x_hbm, xv), (wqkv_hbm, wqkv), (up_hbm, up), (wo_hbm, wo), (down_hbm, down),
             (pp_hbm, ppw), (gqkv_hbm, gqkv), (gout_hbm, gout), (back_hbm, back))
        )
    ]
    for load in loads:
        load.start()

    barrier = pltpu.get_barrier_semaphore()
    peers = [zpeer(d) for d in (1, 2, 3)] + [xpeer(d) for d in (1, 2, 3)] + [y_up, y_down, sibling]
    for peer in peers:
        pl.semaphore_signal(barrier, inc=1, device_id=peer, device_id_type=MESH)
    pl.semaphore_wait(barrier, len(peers))

    def remote(src, dst, ss, rs, peer):
        return pltpu.make_async_remote_copy(
            src_ref=src, dst_ref=dst, send_sem=ss, recv_sem=rs, device_id=peer, device_id_type=MESH
        )

    def pp_copy(c, d):
        return remote(
            ppsend.at[c, lax.rem(z + d, ZN)], pprecv.at[c, d - 1], pp_s.at[c, d - 1], pp_r.at[c, d - 1], zpeer(d)
        )

    def ag_copy(c, d):
        return remote(pin.at[z, c], pin.at[z, c], ag_s.at[c, d - 1], ag_r.at[c, d - 1], zpeer(d))

    def ag_arrival(c, d):
        piece = pin.at[lax.rem(z + ZN - d, ZN), c]
        return remote(piece, piece, ag_s.at[c, d - 1], ag_r.at[c, d - 1], zpeer(d))

    def bulk_copy(c, d):
        return remote(
            bsend.at[c, lax.rem(z + d, ZN)], brecv.at[c, d - 1], bk_s.at[c, d - 1], bk_r.at[c, d - 1], zpeer(d)
        )

    def finish_patches(c):
        total = ppown[c]
        for d in (1, 2, 3):
            pp_copy(c, d).wait_recv()
            total = total + pprecv[c, d - 1].astype(F32)
        pin[z, c] = total.astype(BF16)
        for d in (2, 1, 3):
            ag_copy(c, d).start()

    row_i = lax.broadcasted_iota(jnp.int32, (rows, rows), 0)
    col_i = lax.broadcasted_iota(jnp.int32, (rows, rows), 1)
    to_byte_major = jnp.where(
        col_i == lax.rem(row_i, span) * 8 + row_i // span, 1.0, 0.0
    ).astype(BF16)

    def chunk(c, carry):
        @pl.when(c == 0)
        def _():
            loads[0].wait()
            loads[1].wait()

        xp = dot(to_byte_major, xv[pl.ds(pl.multiple_of(c * rows, rows), rows), :])
        normed = (
            xp * lax.rsqrt(jnp.mean(xp * xp, axis=-1, keepdims=True) + EPS) * gain_ref[...]
        ).astype(BF16)
        q2 = dot(normed, wqkv[0])
        k2 = dot(normed, wqkv[1])
        v2 = dot(normed, wqkv[2]).astype(BF16)
        rr = lax.broadcasted_iota(jnp.int32, (rows, rows), 0)
        cc = lax.broadcasted_iota(jnp.int32, (rows, rows), 1)
        seen = (lax.rem(rr, span) == lax.rem(cc, span)) & (cc // span <= rr // span)
        heads = []
        for h in range(2):
            cut = slice(h * HD, (h + 1) * HD)
            scores = dot_t(unit(q2[:, cut]).astype(BF16), unit(k2[:, cut]).astype(BF16))
            scores = jnp.where(seen, scores * (lscale_ref[h] / math.sqrt(HD)), NEG)
            e = jnp.exp(scores - jnp.max(scores, axis=-1, keepdims=True))
            total = jnp.sum(e, axis=-1, keepdims=True)
            heads.append((dot(e.astype(BF16), v2[:, cut]) / total).astype(BF16))
        lo = jnp.concatenate(heads, axis=1)

        @pl.when(c == 0)
        def _():
            loads[2].wait()

        for n in range(up.shape[1] // 256):
            cut = slice(n * 256, (n + 1) * 256)
            act[:, cut] = jax.nn.gelu(dot(normed, up[:, cut]), approximate=True).astype(BF16)

        @pl.when(c == 0)
        def _():
            loads[3].wait()
            loads[4].wait()
            loads[5].wait()

        mine = lax.broadcasted_iota(jnp.int32, (rows, 1), 0) // own == z
        a = act[...]
        for n in range(part.shape[1] // 256):
            cut = slice(n * 256, (n + 1) * 256)
            t = dot(lo, wo[:, cut]) + dot(a, down[:, cut])
            t = t + jnp.where(mine, xp[:, cut], 0.0)
            part[:, cut] = t
            tb = t.astype(BF16)
            for h in range(ZN):
                bsend[c, h, :, cut] = tb[h * own : (h + 1) * own]
        ownf[c] = part[pl.ds(pl.multiple_of(z * own, own), own), :]
        pp = dot(bsend[c].reshape(rows, part.shape[1]), ppw[...])
        ppf[...] = pp
        pb = pp.astype(BF16)
        gp = pp.shape[1]
        for h in range(ZN):
            for b in range(2):
                at = (2 * h + b) * span
                ppsend[c, h, :, b * gp : (b + 1) * gp] = pb[at : at + span]
        for b in range(2):
            at = pl.multiple_of(z * own + b * span, span)
            ppown[c, :, b * gp : (b + 1) * gp] = ppf[pl.ds(at, span), :]
        for d in (2, 1, 3):
            pp_copy(c, d).start()

        @pl.when(c >= 1)
        def _():
            finish_patches(c - 1)

        @pl.when(c < EARLY)
        def _():
            for d in (2, 1, 3):
                bulk_copy(c, d).start()

        return carry

    lax.fori_loop(0, CHUNKS, chunk, 0)
    finish_patches(CHUNKS - 1)
    for c in range(EARLY, CHUNKS):
        for d in (2, 1, 3):
            bulk_copy(c, d).start()

    loads[6].wait()
    for c in range(CHUNKS):
        for d in (1, 2, 3):
            ag_arrival(c, d).wait_recv()
    patches = CHUNKS * span
    piece = pin.shape[3]
    square = jnp.zeros((patches, 1), F32)
    for h in range(ZN):
        v = pin[h].reshape(patches, piece).astype(F32)
        square = square + jnp.sum(v * v, axis=-1, keepdims=True)
    inv = lax.rsqrt(square / (ZN * piece) + EPS)
    for h in range(ZN):
        cut = slice(h * piece, (h + 1) * piece)
        v = pin[h].reshape(patches, piece).astype(F32)
        gn[:, cut] = (v * inv * ggain_ref[:, cut]).astype(BF16)
    g = gn[...]

    def project(j):
        for half in range(2):
            r = dot(g, gqkv[j, :, half * 256 : (half + 1) * 256])
            for t in range(2):
                v = r[:, t * HD : (t + 1) * HD]
                if j < 2:
                    v = unit(v)
                qkvs[half * 2 + t, j] = v.astype(BF16)

    def xk_copy(d):
        h = lax.rem(x + d, XN)
        return remote(qkvs.at[h, pl.ds(1, 2)], kvbuf.at[y, core, x], xk_s.at[d - 1], xk_r.at[d - 1], xpeer(d))

    def xk_arrival(d):
        at = kvbuf.at[y, core, lax.rem(x + XN - d, XN)]
        return remote(at, at, xk_s.at[d - 1], xk_r.at[d - 1], xpeer(d))

    def xq_copy(d):
        h = lax.rem(x + d, XN)
        return remote(qkvs.at[h, 0], qbuf.at[x], xq_s.at[d - 1], xq_r.at[d - 1], xpeer(d))

    def xq_arrival(d):
        at = qbuf.at[lax.rem(x + XN - d, XN)]
        return remote(at, at, xq_s.at[d - 1], xq_r.at[d - 1], xpeer(d))

    project(1)
    project(2)
    for d in (2, 1, 3):
        xk_copy(d).start()
    kvbuf[y, core, x] = qkvs[x, 1:3]
    project(0)
    for d in (2, 1, 3):
        xq_copy(d).start()
    qbuf[x] = qkvs[x, 0]
    y1 = lax.rem(y + 1, YN)
    y2 = lax.rem(y + 2, YN)
    y3 = lax.rem(y + 3, YN)
    other = 1 - core
    low, high = pl.ds(0, 2), pl.ds(2, 2)

    def same(ref, ss, rs, peer):
        return remote(ref, ref, ss, rs, peer)

    own_up = same(kvbuf.at[y, core], y_s.at[0], y_r.at[0], y_up)
    own_down = same(kvbuf.at[y, core], y_s.at[1], y_r.at[1], y_down)
    relay_up = same(kvbuf.at[y3, core, low], y_s.at[2], y_r.at[2], y_up)
    relay_down = same(kvbuf.at[y1, core, high], y_s.at[3], y_r.at[3], y_down)
    from_down = same(kvbuf.at[y3, core], y_s.at[0], y_r.at[0], y_up)
    from_up = same(kvbuf.at[y1, core], y_s.at[1], y_r.at[1], y_down)
    far_low = same(kvbuf.at[y2, core, low], y_s.at[2], y_r.at[2], y_up)
    far_high = same(kvbuf.at[y2, core, high], y_s.at[3], y_r.at[3], y_down)
    give = [
        same(kvbuf.at[y, core], c_s.at[0], c_r.at[0], sibling),
        same(kvbuf.at[y3, core], c_s.at[1], c_r.at[1], sibling),
        same(kvbuf.at[y1, core], c_s.at[2], c_r.at[2], sibling),
        same(kvbuf.at[y2, core, low], c_s.at[3], c_r.at[3], sibling),
        same(kvbuf.at[y2, core, high], c_s.at[4], c_r.at[4], sibling),
    ]
    get = [
        same(kvbuf.at[y, other], c_s.at[0], c_r.at[0], sibling),
        same(kvbuf.at[y3, other], c_s.at[1], c_r.at[1], sibling),
        same(kvbuf.at[y1, other], c_s.at[2], c_r.at[2], sibling),
        same(kvbuf.at[y2, other, low], c_s.at[3], c_r.at[3], sibling),
        same(kvbuf.at[y2, other, high], c_s.at[4], c_r.at[4], sibling),
    ]

    for d in (1, 3, 2):
        xk_arrival(d).wait_recv()
    own_up.start()
    own_down.start()
    give[0].start()
    for d in (1, 3, 2):
        xq_arrival(d).wait_recv()

    m_ref[...] = jnp.full(m_ref.shape, NEG, F32)
    l_ref[...] = jnp.zeros(l_ref.shape, F32)
    acc[...] = jnp.zeros(acc.shape, F32)
    factor = gscale_ref[x] / math.sqrt(HD)
    keys = XN * patches

    def attend(yb, masked):
        def one(cb, qb):
            k = kvbuf[yb, cb, :, 0].reshape(keys, HD)
            v = kvbuf[yb, cb, :, 1].reshape(keys, HD)
            scores = dot_t(qbuf[qb], k)
            if masked:
                kk = lax.broadcasted_iota(jnp.int32, scores.shape, 1)
                qq = lax.broadcasted_iota(jnp.int32, scores.shape, 0)
                k_at = (2 * (kk // patches) + cb) * patches + lax.rem(kk, patches)
                q_at = (2 * qb + core) * patches + qq
                scores = jnp.where(k_at <= q_at, scores, NEG)
            old = m_ref[qb]
            new = jnp.maximum(old, jnp.max(scores, axis=-1, keepdims=True))
            keep = jnp.exp((old - new) * factor)
            e = jnp.exp((scores - new) * factor)
            m_ref[qb] = new
            l_ref[qb] = l_ref[qb] * keep + jnp.sum(e, axis=-1, keepdims=True)
            acc[qb] = acc[qb] * keep + dot(e.astype(BF16), v)

        return one

    def run(yb, cb, masked):
        one = attend(yb, masked)

        def body(qb, carry):
            one(cb, qb)
            return carry

        lax.fori_loop(0, XN, body, 0)

    def run_both(yb):
        one = attend(yb, False)

        def body(i, carry):
            one(i // XN, lax.rem(i, XN))
            return carry

        @pl.when(yb < y)
        def _():
            lax.fori_loop(0, 2 * XN, body, 0)

    run(y, core, True)
    get[0].wait_recv()
    from_down.wait_recv()
    relay_up.start()
    give[1].start()
    from_up.wait_recv()
    relay_down.start()
    give[2].start()
    run(y, other, True)
    get[1].wait_recv()
    run_both(y3)
    get[2].wait_recv()
    run_both(y1)
    far_low.wait_recv()
    give[3].start()
    far_high.wait_recv()
    give[4].start()
    get[3].wait_recv()
    get[4].wait_recv()
    run_both(y2)

    def o_copy(d):
        h = lax.rem(x + d, XN)
        return remote(osend.at[h], orecv.at[x], o_s.at[d - 1], o_r.at[d - 1], xpeer(d))

    def o_arrival(d):
        at = orecv.at[lax.rem(x + XN - d, XN)]
        return remote(at, at, o_s.at[d - 1], o_r.at[d - 1], xpeer(d))

    for qb in range(XN):
        osend[qb] = (acc[qb] / l_ref[qb]).astype(BF16)
    for d in (2, 1, 3):
        o_copy(d).start()
    orecv[x] = osend[x]
    loads[7].wait()
    for d in (1, 3, 2):
        o_arrival(d).wait_recv()
    gattn = jnp.concatenate([orecv[h] for h in range(XN)], axis=1)

    def out_part(zz):
        return dot(gattn, gout[:, pl.ds(pl.multiple_of(zz * piece, piece), piece)])

    def r_copy(d):
        return remote(rsend.at[d - 1], rrecv.at[d - 1], r_s.at[d - 1], r_r.at[d - 1], zpeer(d))

    for d in (2, 1, 3):
        rsend[d - 1] = out_part(lax.rem(z + d, ZN)).astype(BF16)
        r_copy(d).start()
    update = out_part(z)

    for c in range(CHUNKS):
        state = ownf[c]
        for d in (1, 2, 3):
            bulk_copy(c, d).wait_recv()
            state = state + brecv[c, d - 1].astype(F32)
        state = state.astype(BF16)
        for b in range(2):
            bst[b, c * span : (c + 1) * span] = state[b * span : (b + 1) * span]

    sources, blocks = owners_ref.shape
    spread = jnp.where(
        lax.broadcasted_iota(jnp.int32, (blocks, patches), 1) // 2
        == lax.broadcasted_iota(jnp.int32, (blocks, patches), 0),
        1.0,
        0.0,
    ).astype(BF16)
    listed = dot(owners_ref[...].astype(F32).astype(BF16), spread)
    is_mine = lax.broadcasted_iota(jnp.int32, listed.shape, 0) == s
    listed_row = jnp.sum(jnp.where(is_mine, listed, 0.0), axis=0, keepdims=True)
    pr = lax.broadcasted_iota(jnp.int32, (patches, patches), 0)
    pc = lax.broadcasted_iota(jnp.int32, (patches, patches), 1)
    listed_col = jnp.sum(jnp.where(pr == pc, listed_row, 0.0), axis=1, keepdims=True)
    earlier = (listed_col == listed_row) & (pr < pc) & (lax.rem(pr, 2) == lax.rem(pc, 2))
    rank = jnp.sum(jnp.where(earlier, 1.0, 0.0), axis=0, keepdims=True)
    slot = listed_row * 4.0 + rank * 2.0 + lax.rem(pc, 2).astype(F32)
    pick = jnp.where(slot == pr.astype(F32), 1.0, 0.0).astype(BF16)

    loads[8].wait()
    total = update + pin[z].reshape(patches, piece).astype(F32)
    for d in (1, 3, 2):
        r_copy(d).wait_recv()
        total = total + rrecv[d - 1].astype(F32)
    result = total.astype(BF16)
    perm_ref[...] = dot(pick, result).astype(BF16)
    gp = back.shape[0]
    for b in range(2):
        byte_ref[b] = (
            bst[b].astype(F32) + dot(result[:, b * gp : (b + 1) * gp], back[...])
        ).astype(BF16)

    def drain(c, carry):
        for d in (1, 2, 3):
            pp_copy(c, d).wait_send()
            ag_copy(c, d).wait_send()
            bulk_copy(c, d).wait_send()
        return carry

    lax.fori_loop(0, CHUNKS, drain, 0)
    for d in (1, 2, 3):
        xk_copy(d).wait_send()
        xq_copy(d).wait_send()
        o_copy(d).wait_send()
        r_copy(d).wait_send()
    for copy in (own_up, own_down, relay_up, relay_down, *give):
        copy.wait_send()


def on_device(
    byte_in, local_gain, local_qkv, local_out, mlp_up, mlp_down, local_scale, patch_proj,
    global_gain, global_qkv, global_out, global_scale, back_proj, owners,
):
    patches, span8, dl = byte_in.shape
    gw = global_out.shape[1]
    piece = gw // ZN
    ff = mlp_up.shape[1]
    rows = patches * span8 // CHUNKS
    span = patches // CHUNKS
    own = 2 * span
    gp = back_proj.shape[0]
    wqkv3 = jnp.transpose(local_qkv, (1, 0, 2))
    gqkv3 = jnp.transpose(global_qkv, (1, 0, 2))
    hbm = pl.BlockSpec(memory_space=pl.ANY)
    vm = pl.BlockSpec(memory_space=pltpu.VMEM)
    sm = pl.BlockSpec(memory_space=pltpu.SMEM)
    dma = pltpu.SemaphoreType.DMA

    def buf(*shape, dtype=BF16):
        return pltpu.VMEM(shape, dtype)

    big = [byte_in.reshape(patches * span8, dl), wqkv3, local_out, mlp_up, mlp_down, patch_proj, gqkv3, global_out, back_proj]
    scratch = [buf(*a.shape) for a in big] + [
        buf(rows, ff),
        buf(rows, dl, dtype=F32),
        buf(rows, gp, dtype=F32),
        buf(CHUNKS, ZN, own, dl),
        buf(CHUNKS, ZN - 1, own, dl),
        buf(CHUNKS, own, dl, dtype=F32),
        buf(CHUNKS, ZN, span, 2 * gp),
        buf(CHUNKS, ZN - 1, span, 2 * gp),
        buf(CHUNKS, span, 2 * gp, dtype=F32),
        buf(ZN, CHUNKS, span, piece),
        buf(patches, gw),
        buf(XN, 3, patches, HD),
        buf(YN, 2, XN, 2, patches, HD),
        buf(XN, patches, HD),
        buf(XN, patches, 1, dtype=F32),
        buf(XN, patches, 1, dtype=F32),
        buf(XN, patches, HD, dtype=F32),
        buf(XN, patches, HD),
        buf(XN, patches, HD),
        buf(ZN - 1, patches, piece),
        buf(ZN - 1, patches, piece),
        buf(2, patches, dl),
        dma((9,)),
    ]
    scratch += [dma((CHUNKS, 3))] * 6 + [dma((3,))] * 4 + [dma((4,))] * 2 + [dma((5,))] * 2 + [dma((3,))] * 4
    byte_out, permuted = pl.pallas_call(
        kernel,
        out_shape=(
            jax.ShapeDtypeStruct((2, patches, dl), BF16),
            jax.ShapeDtypeStruct((patches, piece), BF16),
        ),
        in_specs=[hbm] * 9 + [vm] * 3 + [sm] * 2,
        out_specs=(vm, vm),
        scratch_shapes=scratch,
        compiler_params=pltpu.CompilerParams(
            collective_id=0, has_side_effects=True, vmem_limit_bytes=60 * 1024 * 1024
        ),
    )(*big, local_gain.reshape(1, dl), global_gain.reshape(1, gw), owners, local_scale, global_scale)
    global_state = lax.all_to_all(permuted, "seq", split_axis=0, concat_axis=0, tiled=True)
    return (jnp.transpose(byte_out, (1, 0, 2)), global_state)


def solution(mesh):
    placed = (
        P("seq", None, None),
        P(),
        P(None, None, "head"),
        P("head", None),
        P(None, "head"),
        P("head", None),
        P("head"),
        P(),
        P(),
        P(None, None, "head"),
        P("head", None),
        P("head"),
        P(),
        P(),
    )
    return jax.shard_map(
        on_device,
        mesh=mesh,
        in_specs=placed,
        out_specs=(P("seq", "head", None), P("seq", "head")),
        check_vma=False,
    )
```

time: 248 us -> 96.4 us (0.39)
  waiting for transfers between devices: 106 us -> 5.23 us
  Pallas kernels: 0 us -> 70.8 us
  local copies, waits for them, and re-layouts: 53.7 us -> 4.66 us
  matrix products: 35.2 us -> 0 us
  other arithmetic: 15.7 us -> 0 us
  between operations: 15.1 us -> 0.65 us
  blocking collectives: 9.9 us -> 0 us
  starting transfers between devices: 10.8 us -> 14.7 us
    pallas_call x0 -> x1, Pallas kernels: none -> 70.8 us  [on_device(): pl.pallas_call(kernel, out_shape=(jax.ShapeDtypeStruct((2, patches, dl),...]
    all_gather x1 -> x0, waiting for transfers between devices: 52.8 us -> none  [sent_together(): whole, at, outs = (lax.all_gather(both, axis, axis=dim, tiled=True), 0, [])]
    reduce_scatter x1 -> x0, waiting for transfers between devices: 39.3 us -> none  [on_device(): lax.psum_scatter(partial_sum.reshape(patches, patch_span, model_width), '...]
    dot_general x10 -> x0, matrix products: 35.2 us -> none  [the longest x1 8.8 us: on_device(): jnp.dot(activated, mlp_down, preferred_element_type=jnp.float32)]
    another operation x1 -> x0, local copies, waits for them, and re-layouts: 11.5 us -> none
    slice x7 -> x0, local copies, waits for them, and re-layouts: 11.1 us -> none  [the longest x1 3.89 us: sent_together(): outs.append(lax.slice_in_dim(whole, at, at + a.shape[along], axis=along))]
    all_gather x1 -> x0, blocking collectives: 9.9 us -> none  [on_device(): patch_in = lax.all_gather(own_patch, 'head', axis=1, tiled=True)]
    unnamed x16 -> x1, local copies, waits for them, and re-layouts: 11.5 us -> 2.37 us
  transfers between devices with their start and end apart: 4 -> 1, of which waited for: 4 -> 1; matrix products, arithmetic and copies ran while one was open for 7% -> 2% of each run, Pallas kernels for 0% -> 0%
where the time goes in v1:
time: 96.4 us; the launch traced here: 96.1 us
  Pallas kernels  70.8 us (73%)
  starting transfers between devices  14.7 us (15%)
  waiting for transfers between devices  5.23 us (5%)
  local copies, waits for them, and re-layouts  4.66 us (5%)
    pallas_call x1, Pallas kernels, on_device(): pl.pallas_call(kernel, out_shape=(jax.ShapeDtypeStruct((2, patches, dl),...  70.8 us
    all_to_all x1, starting transfers between devices, on_device(): lax.all_to_all(permuted, 'seq', split_axis=0, concat_axis=0, tiled=True)  14.7 us
    all_to_all x1, waiting for transfers between devices, on_device(): lax.all_to_all(permuted, 'seq', split_axis=0, concat_axis=0, tiled=True)  5.23 us
    unnamed x1, local copies, waits for them, and re-layouts  2.37 us
    all_to_all x2, local copies, waits for them, and re-layouts, on_device(): lax.all_to_all(permuted, 'seq', split_axis=0, concat_axis=0, tiled=True)  2.29 us
  transfers between devices with their start and end apart: 1, of which 1 were waited for; matrix products, arithmetic and copies ran while one was open for 2% of the time, Pallas kernels for 0%

profile of v1, /device:TPU:1, one launch (start us, length us, event | category | flops | bytes accessed | tf_op | source)
XLA Modules:
  0.0 96.1 jit_solution(7705998469939567741)
XLA Ops:
  0.6 70.8 %shard_map.149 = (bf16[2,128,1024]{2,1,0:T(8,128)(2,1)}, bf16[128,512]{1,0:T(8,128)(2,1)}) custom-call(bf16[1024,1024]{1,0:T(8,128)(2,1)} %bitcast.7, bf16[3,1024,256]{2,1,0:T(8,128)(2,1)} %bitcast.8, bf16[256,1024]{1,0:T(8,128)(2,1)} %wo_hbm.1, bf16[1024,1024]{1,0:T(8,128)(2,1)} %up_hbm.1, bf16[1024,1024]{1,0:T(8,128)(2,1)} %down_hbm.1, ...), custom_call_target="tpu_custom_call" | custom-call | tf_op jit(solution)/shard_map/pallas_call | solution.py:497
  71.5 1.6 %all_to_all.8 = bf16[32,4,512]{2,1,0:T(4,128)(2,1)} reshape(bf16[128,512]{1,0:T(8,128)(2,1)} %get-tuple-element.5) | data formatting | bytes 262144 | tf_op jit(solution)/shard_map/all_to_all | solution.py:510
  73.1 14.7 %all-to-all-start = ((bf16[32,4,512]{2,1,0:T(4,128)(2,1)}), bf16[32,4,512]{2,1,0:T(4,128)(2,1)S(1)}, u32[]{:S(2)}, u32[]{:S(2)}) async-start(bf16[32,4,512]{2,1,0:T(4,128)(2,1)} %all_to_all.8), calls=%async_computation | async-start | bytes 262144 | tf_op jit(solution)/shard_map/all_to_all | solution.py:510
  87.8 2.4 %copy.16 = bf16[128,2,1024]{2,1,0:T(2,128)(2,1)} copy(bf16[128,2,1024]{2,0,1:T(8,128)(2,1)} %bitcast.9) | data formatting | bytes 1048576
  90.1 5.2 %all-to-all-done = bf16[32,4,512]{2,1,0:T(4,128)(2,1)S(1)} async-done(((bf16[32,4,512]{2,1,0:T(4,128)(2,1)}), bf16[32,4,512]{2,1,0:T(4,128)(2,1)S(1)}, u32[]{:S(2)}, u32[]{:S(2)}) %all-to-all-start) | async-done | bytes 131104 | tf_op jit(solution)/shard_map/all_to_all | solution.py:510
  95.4 0.7 all_to_all.10
Async XLA Ops:
  73.1 22.3 %all-to-all-start = ((bf16[32,4,512]{2,1,0:T(4,128)(2,1)}), bf16[32,4,512]{2,1,0:T(4,128)(2,1)S(1)}, u32[]{:S(2)}, u32[]{:S(2)}) async-start(bf16[32,4,512]{2,1,0:T(4,128)(2,1)} %all_to_all.8), calls=%async_computation | async-start | bytes 262144 | tf_op jit(solution)/shard_map/all_to_all | solution.py:510

commit v2 on v1

--- a/solution.py
+++ b/solution.py
@@ -36,12 +36,12 @@
 def kernel(
     x_hbm, wqkv_hbm, wo_hbm, up_hbm, down_hbm, pp_hbm, gqkv_hbm, gout_hbm, back_hbm,
     gain_ref, ggain_ref, owners_ref, lscale_ref, gscale_ref,
-    byte_ref, perm_ref,
+    byte_ref, state_ref,
     xv, wqkv, wo, up, down, ppw, gqkv, gout, back,
     act, part, ppf, bsend, brecv, ownf, ppsend, pprecv, ppown, pin,
-    gn, qkvs, kvbuf, qbuf, m_ref, l_ref, acc, osend, orecv, rsend, rrecv, bst,
+    gn, qkvs, kvbuf, qbuf, m_ref, l_ref, acc, osend, orecv, rsend, rrecv, bst, psend,
     lsem, pp_s, pp_r, ag_s, ag_r, bk_s, bk_r, xk_s, xk_r, xq_s, xq_r,
-    y_s, y_r, c_s, c_r, o_s, o_r, r_s, r_r,
+    y_s, y_r, c_s, c_r, o_s, o_r, r_s, r_r, p_s, p_r,
 ):
     s = lax.axis_index("seq")
     z = lax.axis_index("head")
@@ -76,10 +76,19 @@
         load.start()
 
     barrier = pltpu.get_barrier_semaphore()
-    peers = [zpeer(d) for d in (1, 2, 3)] + [xpeer(d) for d in (1, 2, 3)] + [y_up, y_down, sibling]
-    for peer in peers:
+    plane = 2 * XN * YN
+
+    def greet(peer):
         pl.semaphore_signal(barrier, inc=1, device_id=peer, device_id_type=MESH)
-    pl.semaphore_wait(barrier, len(peers))
+
+    def greet_plane(d, carry):
+        greet((lax.rem(s + d, plane), z))
+        return carry
+
+    for d in (1, 2, 3):
+        greet(zpeer(d))
+    lax.fori_loop(1, plane, greet_plane, 0)
+    pl.semaphore_wait(barrier, ZN - 1 + plane - 1)
 
     def remote(src, dst, ss, rs, peer):
         return pltpu.make_async_remote_copy(
@@ -388,14 +397,15 @@
         r_copy(d).start()
     update = out_part(z)
 
+    ri = lax.broadcasted_iota(jnp.int32, (own, own), 0)
+    ci = lax.broadcasted_iota(jnp.int32, (own, own), 1)
+    to_patch_major = jnp.where(ci == lax.rem(ri, 2) * span + ri // 2, 1.0, 0.0).astype(BF16)
     for c in range(CHUNKS):
         state = ownf[c]
         for d in (1, 2, 3):
             bulk_copy(c, d).wait_recv()
             state = state + brecv[c, d - 1].astype(F32)
-        state = state.astype(BF16)
-        for b in range(2):
-            bst[b, c * span : (c + 1) * span] = state[b * span : (b + 1) * span]
+        bst[c * own : (c + 1) * own] = dot(to_patch_major, state.astype(BF16)).astype(BF16)
 
     sources, blocks = owners_ref.shape
     spread = jnp.where(
@@ -415,18 +425,47 @@
     slot = listed_row * 4.0 + rank * 2.0 + lax.rem(pc, 2).astype(F32)
     pick = jnp.where(slot == pr.astype(F32), 1.0, 0.0).astype(BF16)
 
+    per = patches // plane
     loads[8].wait()
     total = update + pin[z].reshape(patches, piece).astype(F32)
     for d in (1, 3, 2):
         r_copy(d).wait_recv()
         total = total + rrecv[d - 1].astype(F32)
     result = total.astype(BF16)
-    perm_ref[...] = dot(pick, result).astype(BF16)
+    sorted_rows = dot(pick, result)
+    for o in range(plane):
+        psend[o] = sorted_rows[o * per : (o + 1) * per].astype(BF16)
+
+    def p_copy(d):
+        return remote(
+            psend.at[lax.rem(s + d, plane)], state_ref.at[s], p_s.at[d - 1], p_r.at[d - 1], (lax.rem(s + d, plane), z)
+        )
+
+    def p_start(d, carry):
+        p_copy(d).start()
+        return carry
+
+    lax.fori_loop(1, plane, p_start, 0)
+    state_ref[s] = psend[s]
     gp = back.shape[0]
+    re = lax.broadcasted_iota(jnp.int32, (2 * patches, patches), 0)
+    ce = lax.broadcasted_iota(jnp.int32, (2 * patches, patches), 1)
+    shares = jnp.zeros((2 * patches, gp), F32)
     for b in range(2):
-        byte_ref[b] = (
-            bst[b].astype(F32) + dot(result[:, b * gp : (b + 1) * gp], back[...])
-        ).astype(BF16)
+        lift = jnp.where(re == 2 * ce + b, 1.0, 0.0).astype(BF16)
+        shares = shares + dot(lift, result[:, b * gp : (b + 1) * gp])
+    shares = shares.astype(BF16)
+    for n in range(bst.shape[1] // 256):
+        cut = slice(n * 256, (n + 1) * 256)
+        byte_ref[:, cut] = (bst[:, cut].astype(F32) + dot(shares, back[:, cut])).astype(BF16)
+
+    def p_wait(d, carry):
+        at = state_ref.at[lax.rem(s + plane - d, plane)]
+        remote(at, at, p_s.at[d - 1], p_r.at[d - 1], (lax.rem(s + d, plane), z)).wait_recv()
+        p_copy(d).wait_send()
+        return carry
+
+    lax.fori_loop(1, plane, p_wait, 0)
 
     def drain(c, carry):
         for d in (1, 2, 3):
@@ -457,6 +496,7 @@
     span = patches // CHUNKS
     own = 2 * span
     gp = back_proj.shape[0]
+    plane = 2 * XN * YN
     wqkv3 = jnp.transpose(local_qkv, (1, 0, 2))
     gqkv3 = jnp.transpose(global_qkv, (1, 0, 2))
     hbm = pl.BlockSpec(memory_space=pl.ANY)
@@ -490,15 +530,16 @@
         buf(XN, patches, HD),
         buf(ZN - 1, patches, piece),
         buf(ZN - 1, patches, piece),
-        buf(2, patches, dl),
+        buf(2 * patches, dl),
+        buf(plane, patches // plane, piece),
         dma((9,)),
     ]
-    scratch += [dma((CHUNKS, 3))] * 6 + [dma((3,))] * 4 + [dma((4,))] * 2 + [dma((5,))] * 2 + [dma((3,))] * 4
-    byte_out, permuted = pl.pallas_call(
+    scratch += [dma((CHUNKS, 3))] * 6 + [dma((3,))] * 4 + [dma((4,))] * 2 + [dma((5,))] * 2 + [dma((3,))] * 4 + [dma((plane - 1,))] * 2
+    byte_out, global_state = pl.pallas_call(
         kernel,
         out_shape=(
-            jax.ShapeDtypeStruct((2, patches, dl), BF16),
-            jax.ShapeDtypeStruct((patches, piece), BF16),
+            jax.ShapeDtypeStruct((2 * patches, dl), BF16),
+            jax.ShapeDtypeStruct((plane, patches // plane, piece), BF16),
         ),
         in_specs=[hbm] * 9 + [vm] * 3 + [sm] * 2,
         out_specs=(vm, vm),
@@ -507,8 +548,7 @@
             collective_id=0, has_side_effects=True, vmem_limit_bytes=60 * 1024 * 1024
         ),
     )(*big, local_gain.reshape(1, dl), global_gain.reshape(1, gw), owners, local_scale, global_scale)
-    global_state = lax.all_to_all(permuted, "seq", split_axis=0, concat_axis=0, tiled=True)
-    return (jnp.transpose(byte_out, (1, 0, 2)), global_state)
+    return (byte_out.reshape(patches, 2, dl), global_state.reshape(patches, piece))
 
 
 def solution(mesh):

time: 96.4 us -> 93.1 us (0.966)
  Pallas kernels: 70.8 us -> 88.6 us
  starting transfers between devices: 14.7 us -> 0 us
  waiting for transfers between devices: 5.23 us -> 0 us
  local copies, waits for them, and re-layouts: 4.66 us -> 3.63 us
    pallas_call x1, Pallas kernels: 70.8 us -> 88.6 us  [on_device(): pl.pallas_call(kernel, out_shape=(jax.ShapeDtypeStruct((2 * patches, dl),...]
    all_to_all x1 -> x0, starting transfers between devices: 14.7 us -> none  [on_device(): lax.all_to_all(permuted, 'seq', split_axis=0, concat_axis=0, tiled=True)]
    all_to_all x1 -> x0, waiting for transfers between devices: 5.23 us -> none  [on_device(): lax.all_to_all(permuted, 'seq', split_axis=0, concat_axis=0, tiled=True)]
    reshape x0 -> x2, local copies, waits for them, and re-layouts: none -> 3.63 us  [the longest x1 2.03 us: on_device(): byte_out.reshape(patches, 2, dl)]
    unnamed x1 -> x0, local copies, waits for them, and re-layouts: 2.37 us -> none
    all_to_all x2 -> x0, local copies, waits for them, and re-layouts: 2.29 us -> none  [on_device(): lax.all_to_all(permuted, 'seq', split_axis=0, concat_axis=0, tiled=True)]
  transfers between devices with their start and end apart: 1 -> 0, of which waited for: 1 -> 0; matrix products, arithmetic and copies ran while one was open for 2% -> 0% of each run, Pallas kernels for 0% -> 0%
where the time goes in v2:
time: 93.1 us; the launch traced here: 92.9 us
  Pallas kernels  88.6 us (95%)
  local copies, waits for them, and re-layouts  3.63 us (4%)
    pallas_call x1, Pallas kernels, on_device(): pl.pallas_call(kernel, out_shape=(jax.ShapeDtypeStruct((2 * patches, dl),...  88.6 us
    reshape x1, local copies, waits for them, and re-layouts, on_device(): byte_out.reshape(patches, 2, dl)  2.03 us

profile of v2, /device:TPU:1, one launch (start us, length us, event | category | flops | bytes accessed | tf_op | source)
XLA Modules:
  0.0 92.9 jit_solution(13307170107615764399)
XLA Ops:
  0.6 88.6 %shard_map.149 = (bf16[256,1024]{1,0:T(8,128)(2,1)}, bf16[32,4,512]{2,1,0:T(4,128)(2,1)}) custom-call(bf16[1024,1024]{1,0:T(8,128)(2,1)} %bitcast.6, bf16[3,1024,256]{2,1,0:T(8,128)(2,1)} %bitcast.7, bf16[256,1024]{1,0:T(8,128)(2,1)} %wo_hbm.1, bf16[1024,1024]{1,0:T(8,128)(2,1)} %up_hbm.1, bf16[1024,1024]{1,0:T(8,128)(2,1)} %down_hbm.1, ...), custom_call_target="tpu_custom_call" | custom-call | tf_op jit(solution)/shard_map/pallas_call | solution.py:538
  89.3 2.0 %reshape.22 = bf16[128,2,1024]{2,1,0:T(2,128)(2,1)} reshape(bf16[256,1024]{1,0:T(8,128)(2,1)} %get-tuple-element.4) | data formatting | bytes 1048576 | tf_op jit(solution)/shard_map/reshape | solution.py:551
  91.3 1.6 %reshape.23 = bf16[128,512]{1,0:T(8,128)(2,1)} reshape(bf16[32,4,512]{2,1,0:T(4,128)(2,1)} %get-tuple-element.5) | data formatting | bytes 262144 | tf_op jit(solution)/shard_map/reshape | solution.py:551

commit v3 on v2

--- a/solution.py
+++ b/solution.py
@@ -17,7 +17,6 @@
 YN = 4
 ZN = 4
 CHUNKS = 4
-EARLY = 2
 HD = 128
 
 
@@ -38,10 +37,10 @@
     gain_ref, ggain_ref, owners_ref, lscale_ref, gscale_ref,
     byte_ref, state_ref,
     xv, wqkv, wo, up, down, ppw, gqkv, gout, back,
-    act, part, ppf, bsend, brecv, ownf, ppsend, pprecv, ppown, pin,
-    gn, qkvs, kvbuf, qbuf, m_ref, l_ref, acc, osend, orecv, rsend, rrecv, bst, psend,
-    lsem, pp_s, pp_r, ag_s, ag_r, bk_s, bk_r, xk_s, xk_r, xq_s, xq_r,
-    y_s, y_r, c_s, c_r, o_s, o_r, r_s, r_r, p_s, p_r,
+    act, part, ppf, bsend, bfar, brecv, ownf, ppsend, pprecv, ppown, pin,
+    gn, qkvs, kvbuf, qbuf, m_ref, l_ref, acc, opart, oget, stpart, stget, osend, orecv, rfs, rfar, rsend, rrecv, bst, psend,
+    lsem, pp_s, pp_r, ag_s, ag_r, bf_s, bf_r, bk_s, bk_r, xk_s, xk_r, xq_s, xq_r,
+    yu_s, yu_r, yd_s, yd_r, ru_s, ru_r, rd_s, rd_r, c_s, c_r, o_s, o_r, rf_s, rf_r, r_s, r_r, p_s, p_r,
 ):
     s = lax.axis_index("seq")
     z = lax.axis_index("head")
@@ -88,7 +87,6 @@
     for d in (1, 2, 3):
         greet(zpeer(d))
     lax.fori_loop(1, plane, greet_plane, 0)
-    pl.semaphore_wait(barrier, ZN - 1 + plane - 1)
 
     def remote(src, dst, ss, rs, peer):
         return pltpu.make_async_remote_copy(
@@ -107,10 +105,33 @@
         piece = pin.at[lax.rem(z + ZN - d, ZN), c]
         return remote(piece, piece, ag_s.at[c, d - 1], ag_r.at[c, d - 1], zpeer(d))
 
-    def bulk_copy(c, d):
-        return remote(
-            bsend.at[c, lax.rem(z + d, ZN)], brecv.at[c, d - 1], bk_s.at[c, d - 1], bk_r.at[c, d - 1], zpeer(d)
+    z_up = zpeer(1)
+    z_down = zpeer(ZN - 1)
+    up_at = lax.rem(z + 1, ZN)
+    down_at = lax.rem(z + ZN - 1, ZN)
+    far_at = lax.rem(z + 2, ZN)
+
+    def bulk_far(c):
+        return (
+            remote(bsend.at[c, far_at, 0], bfar.at[c, 0], bf_s.at[c, 0], bf_r.at[c, 0], z_up),
+            remote(bsend.at[c, far_at, 1], bfar.at[c, 1], bf_s.at[c, 1], bf_r.at[c, 1], z_down),
         )
+
+    def bulk_up(c, b):
+        return remote(bsend.at[c, up_at, b], brecv.at[c, 0, b], bk_s.at[c, b], bk_r.at[c, b], z_up)
+
+    def bulk_down(c, b):
+        return remote(bsend.at[c, down_at, b], brecv.at[c, 1, b], bk_s.at[c, 2 + b], bk_r.at[c, 2 + b], z_down)
+
+    def bulk_combine(c, carry):
+        far_up, far_down = bulk_far(c)
+        far_up.wait_recv()
+        bsend[c, up_at, 0] = (bsend[c, up_at, 0].astype(F32) + bfar[c, 0].astype(F32)).astype(BF16)
+        bulk_up(c, 0).start()
+        far_down.wait_recv()
+        bsend[c, down_at, 1] = (bsend[c, down_at, 1].astype(F32) + bfar[c, 1].astype(F32)).astype(BF16)
+        bulk_down(c, 1).start()
+        return carry
 
     def finish_patches(c):
         total = ppown[c]
@@ -121,6 +142,8 @@
         for d in (2, 1, 3):
             ag_copy(c, d).start()
 
+    loads[0].wait()
+    loads[1].wait()
     row_i = lax.broadcasted_iota(jnp.int32, (rows, rows), 0)
     col_i = lax.broadcasted_iota(jnp.int32, (rows, rows), 1)
     to_byte_major = jnp.where(
@@ -128,11 +151,6 @@
     ).astype(BF16)
 
     def chunk(c, carry):
-        @pl.when(c == 0)
-        def _():
-            loads[0].wait()
-            loads[1].wait()
-
         xp = dot(to_byte_major, xv[pl.ds(pl.multiple_of(c * rows, rows), rows), :])
         normed = (
             xp * lax.rsqrt(jnp.mean(xp * xp, axis=-1, keepdims=True) + EPS) * gain_ref[...]
@@ -140,6 +158,12 @@
         q2 = dot(normed, wqkv[0])
         k2 = dot(normed, wqkv[1])
         v2 = dot(normed, wqkv[2]).astype(BF16)
+
+        @pl.when(c == 0)
+        def _():
+            for load in loads[2:6]:
+                load.wait()
+
         rr = lax.broadcasted_iota(jnp.int32, (rows, rows), 0)
         cc = lax.broadcasted_iota(jnp.int32, (rows, rows), 1)
         seen = (lax.rem(rr, span) == lax.rem(cc, span)) & (cc // span <= rr // span)
@@ -153,19 +177,9 @@
             heads.append((dot(e.astype(BF16), v2[:, cut]) / total).astype(BF16))
         lo = jnp.concatenate(heads, axis=1)
 
-        @pl.when(c == 0)
-        def _():
-            loads[2].wait()
-
         for n in range(up.shape[1] // 256):
             cut = slice(n * 256, (n + 1) * 256)
             act[:, cut] = jax.nn.gelu(dot(normed, up[:, cut]), approximate=True).astype(BF16)
-
-        @pl.when(c == 0)
-        def _():
-            loads[3].wait()
-            loads[4].wait()
-            loads[5].wait()
 
         mine = lax.broadcasted_iota(jnp.int32, (rows, 1), 0) // own == z
         a = act[...]
@@ -176,7 +190,9 @@
             part[:, cut] = t
             tb = t.astype(BF16)
             for h in range(ZN):
-                bsend[c, h, :, cut] = tb[h * own : (h + 1) * own]
+                for b in range(2):
+                    at = h * own + b * span
+                    bsend[c, h, b, :, cut] = tb[at : at + span]
         ownf[c] = part[pl.ds(pl.multiple_of(z * own, own), own), :]
         pp = dot(bsend[c].reshape(rows, part.shape[1]), ppw[...])
         ppf[...] = pp
@@ -189,6 +205,11 @@
         for b in range(2):
             at = pl.multiple_of(z * own + b * span, span)
             ppown[c, :, b * gp : (b + 1) * gp] = ppf[pl.ds(at, span), :]
+
+        @pl.when(c == 0)
+        def _():
+            pl.semaphore_wait(barrier, ZN - 1 + plane - 1)
+
         for d in (2, 1, 3):
             pp_copy(c, d).start()
 
@@ -196,23 +217,20 @@
         def _():
             finish_patches(c - 1)
 
-        @pl.when(c < EARLY)
-        def _():
-            for d in (2, 1, 3):
-                bulk_copy(c, d).start()
-
         return carry
 
     lax.fori_loop(0, CHUNKS, chunk, 0)
     finish_patches(CHUNKS - 1)
-    for c in range(EARLY, CHUNKS):
-        for d in (2, 1, 3):
-            bulk_copy(c, d).start()
-
     loads[6].wait()
     for c in range(CHUNKS):
         for d in (1, 2, 3):
             ag_arrival(c, d).wait_recv()
+    for c in range(CHUNKS):
+        for copy in bulk_far(c):
+            copy.start()
+    for c in range(CHUNKS):
+        bulk_up(c, 1).start()
+        bulk_down(c, 0).start()
     patches = CHUNKS * span
     piece = pin.shape[3]
     square = jnp.zeros((patches, 1), F32)
@@ -233,140 +251,185 @@
                 v = r[:, t * HD : (t + 1) * HD]
                 if j < 2:
                     v = unit(v)
+                if j == 2:
+                    v = jnp.transpose(v)
                 qkvs[half * 2 + t, j] = v.astype(BF16)
 
     def xk_copy(d):
         h = lax.rem(x + d, XN)
-        return remote(qkvs.at[h, pl.ds(1, 2)], kvbuf.at[y, core, x], xk_s.at[d - 1], xk_r.at[d - 1], xpeer(d))
+        return remote(qkvs.at[h, pl.ds(1, 2)], kvbuf.at[y, x], xk_s.at[d - 1], xk_r.at[d - 1], xpeer(d))
+
+    def src(d):
+        return lax.rem(x + XN - d, XN)
 
     def xk_arrival(d):
-        at = kvbuf.at[y, core, lax.rem(x + XN - d, XN)]
+        at = kvbuf.at[y, src(d)]
         return remote(at, at, xk_s.at[d - 1], xk_r.at[d - 1], xpeer(d))
 
     def xq_copy(d):
         h = lax.rem(x + d, XN)
-        return remote(qkvs.at[h, 0], qbuf.at[x], xq_s.at[d - 1], xq_r.at[d - 1], xpeer(d))
+        return remote(qkvs.at[h, 0], qbuf.at[0, x], xq_s.at[d - 1], xq_r.at[d - 1], xpeer(d))
 
     def xq_arrival(d):
-        at = qbuf.at[lax.rem(x + XN - d, XN)]
+        at = qbuf.at[0, src(d)]
         return remote(at, at, xq_s.at[d - 1], xq_r.at[d - 1], xpeer(d))
+
+    y1 = lax.rem(y + 1, YN)
+    y2 = lax.rem(y + 2, YN)
+    y3 = lax.rem(y + 3, YN)
+
+    def up_copy(row, d, ss, rs):
+        at = kvbuf.at[row, src(d)]
+        return remote(at, at, ss.at[d], rs.at[d], y_up)
+
+    def down_copy(row, d, ss, rs):
+        at = kvbuf.at[row, src(d)]
+        return remote(at, at, ss.at[d], rs.at[d], y_down)
+
+    last = YN - 1
+    inner = (y >= 1) & (y < last)
+    outer = (y == 0) | (y == last)
+
+    def spread_piece(d, act_on):
+        @pl.when(y < last)
+        def _():
+            act_on(up_copy(y, d, yu_s, yu_r))
+
+        @pl.when((y == 0) | ((y == 1) & (d % 2 == 1)))
+        def _():
+            act_on(down_copy(y, d, yd_s, yd_r))
+
+    def start(copy):
+        copy.start()
+
+    def sent(copy):
+        copy.wait_send()
+
+    def take_down(d):
+        @pl.when(y >= 1)
+        def _():
+            up_copy(y3, d, yu_s, yu_r).wait_recv()
+
+        if d % 2 == 0:
+
+            @pl.when(inner)
+            def _():
+                up_copy(y3, d, ru_s, ru_r).start()
+
+    def take_up(d):
+        @pl.when((y == last) | ((y == 0) & (d % 2 == 1)))
+        def _():
+            down_copy(y1, d, yd_s, yd_r).wait_recv()
+
+        if d % 2 == 1:
+
+            @pl.when(outer)
+            def _():
+                down_copy(y1, d, rd_s, rd_r).start()
+
+    def take_far():
+        @pl.when(y >= 2)
+        def _():
+            for d in (0, 2):
+                up_copy(y2, d, ru_s, ru_r).wait_recv()
+            for d in (1, 3):
+                down_copy(y2, d, rd_s, rd_r).wait_recv()
+
+    q_give = remote(qbuf.at[0], qbuf.at[1], c_s.at[0], c_r.at[0], sibling)
+    o_give = remote(opart, oget, c_s.at[1], c_r.at[1], sibling)
+    st_give = remote(stpart, stget, c_s.at[2], c_r.at[2], sibling)
 
     project(1)
     project(2)
     for d in (2, 1, 3):
         xk_copy(d).start()
-    kvbuf[y, core, x] = qkvs[x, 1:3]
+    kvbuf[y, x] = qkvs[x, 1:3]
+    spread_piece(0, start)
     project(0)
     for d in (2, 1, 3):
         xq_copy(d).start()
-    qbuf[x] = qkvs[x, 0]
-    y1 = lax.rem(y + 1, YN)
-    y2 = lax.rem(y + 2, YN)
-    y3 = lax.rem(y + 3, YN)
-    other = 1 - core
-    low, high = pl.ds(0, 2), pl.ds(2, 2)
-
-    def same(ref, ss, rs, peer):
-        return remote(ref, ref, ss, rs, peer)
-
-    own_up = same(kvbuf.at[y, core], y_s.at[0], y_r.at[0], y_up)
-    own_down = same(kvbuf.at[y, core], y_s.at[1], y_r.at[1], y_down)
-    relay_up = same(kvbuf.at[y3, core, low], y_s.at[2], y_r.at[2], y_up)
-    relay_down = same(kvbuf.at[y1, core, high], y_s.at[3], y_r.at[3], y_down)
-    from_down = same(kvbuf.at[y3, core], y_s.at[0], y_r.at[0], y_up)
-    from_up = same(kvbuf.at[y1, core], y_s.at[1], y_r.at[1], y_down)
-    far_low = same(kvbuf.at[y2, core, low], y_s.at[2], y_r.at[2], y_up)
-    far_high = same(kvbuf.at[y2, core, high], y_s.at[3], y_r.at[3], y_down)
-    give = [
-        same(kvbuf.at[y, core], c_s.at[0], c_r.at[0], sibling),
-        same(kvbuf.at[y3, core], c_s.at[1], c_r.at[1], sibling),
-        same(kvbuf.at[y1, core], c_s.at[2], c_r.at[2], sibling),
-        same(kvbuf.at[y2, core, low], c_s.at[3], c_r.at[3], sibling),
-        same(kvbuf.at[y2, core, high], c_s.at[4], c_r.at[4], sibling),
-    ]
-    get = [
-        same(kvbuf.at[y, other], c_s.at[0], c_r.at[0], sibling),
-        same(kvbuf.at[y3, other], c_s.at[1], c_r.at[1], sibling),
-        same(kvbuf.at[y1, other], c_s.at[2], c_r.at[2], sibling),
-        same(kvbuf.at[y2, other, low], c_s.at[3], c_r.at[3], sibling),
-        same(kvbuf.at[y2, other, high], c_s.at[4], c_r.at[4], sibling),
-    ]
-
-    for d in (1, 3, 2):
-        xk_arrival(d).wait_recv()
-    own_up.start()
-    own_down.start()
-    give[0].start()
-    for d in (1, 3, 2):
-        xq_arrival(d).wait_recv()
-
+    qbuf[0, x] = qkvs[x, 0]
     m_ref[...] = jnp.full(m_ref.shape, NEG, F32)
     l_ref[...] = jnp.zeros(l_ref.shape, F32)
     acc[...] = jnp.zeros(acc.shape, F32)
-    factor = gscale_ref[x] / math.sqrt(HD)
-    keys = XN * patches
-
-    def attend(yb, masked):
-        def one(cb, qb):
-            k = kvbuf[yb, cb, :, 0].reshape(keys, HD)
-            v = kvbuf[yb, cb, :, 1].reshape(keys, HD)
-            scores = dot_t(qbuf[qb], k)
+    factor = gscale_ref[x] * (math.log2(math.e) / math.sqrt(HD))
+
+    for d in (1, 3, 2):
+        xk_arrival(d).wait_recv()
+        spread_piece(d, start)
+    for d in (1, 3, 2):
+        xq_arrival(d).wait_recv()
+    q_give.start()
+
+    half_q = XN * patches // 2
+
+    def attend(yb, rel, masked):
+        queries = qbuf[rel].reshape(XN * patches, HD)
+        for part_q in range(2):
+            cut = slice(part_q * half_q, (part_q + 1) * half_q)
+            wide = (part_q + 1) * XN // 2 if masked else XN
+            k = kvbuf[yb, 0:wide, 0].reshape(wide * patches, HD)
+            vt = jnp.concatenate([kvbuf[yb, i, 1] for i in range(wide)], axis=1)
+            scores = dot_t(k, queries[cut])
             if masked:
-                kk = lax.broadcasted_iota(jnp.int32, scores.shape, 1)
-                qq = lax.broadcasted_iota(jnp.int32, scores.shape, 0)
-                k_at = (2 * (kk // patches) + cb) * patches + lax.rem(kk, patches)
-                q_at = (2 * qb + core) * patches + qq
+                kk = lax.broadcasted_iota(jnp.int32, scores.shape, 0)
+                qq = lax.broadcasted_iota(jnp.int32, scores.shape, 1) + part_q * half_q
+                theirs = core + rel * (1 - 2 * core)
+                k_at = kk + (kk // patches + core) * patches
+                q_at = qq + (qq // patches + theirs) * patches
                 scores = jnp.where(k_at <= q_at, scores, NEG)
-            old = m_ref[qb]
-            new = jnp.maximum(old, jnp.max(scores, axis=-1, keepdims=True))
-            keep = jnp.exp((old - new) * factor)
-            e = jnp.exp((scores - new) * factor)
-            m_ref[qb] = new
-            l_ref[qb] = l_ref[qb] * keep + jnp.sum(e, axis=-1, keepdims=True)
-            acc[qb] = acc[qb] * keep + dot(e.astype(BF16), v)
-
-        return one
-
-    def run(yb, cb, masked):
-        one = attend(yb, masked)
-
-        def body(qb, carry):
-            one(cb, qb)
-            return carry
-
-        lax.fori_loop(0, XN, body, 0)
+            old = m_ref[rel, :, cut]
+            new = jnp.maximum(old, jnp.max(scores, axis=0, keepdims=True))
+            keep = jnp.exp2((old - new) * factor)
+            e = jnp.exp2((scores - new) * factor)
+            m_ref[rel, :, cut] = new
+            l_ref[rel, :, cut] = l_ref[rel, :, cut] * keep + jnp.sum(e, axis=0, keepdims=True)
+            acc[rel, :, cut] = acc[rel, :, cut] * keep + dot(vt, e.astype(BF16))
 
     def run_both(yb):
-        one = attend(yb, False)
-
-        def body(i, carry):
-            one(i // XN, lax.rem(i, XN))
-            return carry
-
         @pl.when(yb < y)
         def _():
-            lax.fori_loop(0, 2 * XN, body, 0)
-
-    run(y, core, True)
-    get[0].wait_recv()
-    from_down.wait_recv()
-    relay_up.start()
-    give[1].start()
-    from_up.wait_recv()
-    relay_down.start()
-    give[2].start()
-    run(y, other, True)
-    get[1].wait_recv()
+            def body(i, carry):
+                attend(yb, 1 - i, False)
+                return carry
+
+            lax.fori_loop(0, 2, body, 0)
+
+
+    def own_body(rel, carry):
+        @pl.when(rel == 1)
+        def _():
+            take_down(0)
+            q_give.wait_recv()
+
+        attend(y, rel, True)
+        return carry
+
+    lax.fori_loop(0, 2, own_body, 0)
+    for d in (1, 3, 2):
+        take_down(d)
+    for d in (0, 1, 3, 2):
+        take_up(d)
     run_both(y3)
-    get[2].wait_recv()
     run_both(y1)
-    far_low.wait_recv()
-    give[3].start()
-    far_high.wait_recv()
-    give[4].start()
-    get[3].wait_recv()
-    get[4].wait_recv()
+    lax.fori_loop(0, CHUNKS, bulk_combine, 0)
+    take_far()
     run_both(y2)
+    opart[...] = (acc[1] / l_ref[1]).astype(BF16)
+    stpart[...] = jnp.zeros(stpart.shape, F32)
+    stpart[0:1] = m_ref[1]
+    stpart[1:2] = l_ref[1]
+    o_give.start()
+    st_give.start()
+    o_give.wait_recv()
+    st_give.wait_recv()
+    m0, m1 = m_ref[0], stget[0:1]
+    top = jnp.maximum(m0, m1)
+    w0 = jnp.exp2((m0 - top) * factor)
+    w1 = jnp.exp2((m1 - top) * factor) * stget[1:2]
+    mixed = (acc[0] * w0 + oget[...].astype(F32) * w1) / (l_ref[0] * w0 + w1)
+    for qb in range(XN):
+        osend[qb] = jnp.transpose(mixed[:, qb * patches : (qb + 1) * patches]).astype(BF16)
 
     def o_copy(d):
         h = lax.rem(x + d, XN)
@@ -376,8 +439,6 @@
         at = orecv.at[lax.rem(x + XN - d, XN)]
         return remote(at, at, o_s.at[d - 1], o_r.at[d - 1], xpeer(d))
 
-    for qb in range(XN):
-        osend[qb] = (acc[qb] / l_ref[qb]).astype(BF16)
     for d in (2, 1, 3):
         o_copy(d).start()
     orecv[x] = osend[x]
@@ -389,23 +450,51 @@
     def out_part(zz):
         return dot(gattn, gout[:, pl.ds(pl.multiple_of(zz * piece, piece), piece)])
 
-    def r_copy(d):
-        return remote(rsend.at[d - 1], rrecv.at[d - 1], r_s.at[d - 1], r_r.at[d - 1], zpeer(d))
-
-    for d in (2, 1, 3):
-        rsend[d - 1] = out_part(lax.rem(z + d, ZN)).astype(BF16)
-        r_copy(d).start()
+    half_p = patches // 2
+    low, high = slice(0, half_p), slice(half_p, patches)
+    far_up = remote(rfs.at[0], rfar.at[0], rf_s.at[0], rf_r.at[0], z_up)
+    far_down = remote(rfs.at[1], rfar.at[1], rf_s.at[1], rf_r.at[1], z_down)
+
+    def r_up(b):
+        return remote(rsend.at[0, b], rrecv.at[0, b], r_s.at[b], r_r.at[b], z_up)
+
+    def r_down(b):
+        return remote(rsend.at[1, b], rrecv.at[1, b], r_s.at[2 + b], r_r.at[2 + b], z_down)
+
+    far_part = out_part(far_at).astype(BF16)
+    rfs[0] = far_part[low]
+    far_up.start()
+    rfs[1] = far_part[high]
+    far_down.start()
+    up_part = out_part(up_at)
+    rsend[0, 1] = up_part[high].astype(BF16)
+    r_up(1).start()
+    down_part = out_part(down_at)
+    rsend[1, 0] = down_part[low].astype(BF16)
+    r_down(0).start()
     update = out_part(z)
+    far_up.wait_recv()
+    rsend[0, 0] = (up_part[low] + rfar[0].astype(F32)).astype(BF16)
+    r_up(0).start()
+    far_down.wait_recv()
+    rsend[1, 1] = (down_part[high] + rfar[1].astype(F32)).astype(BF16)
+    r_down(1).start()
 
     ri = lax.broadcasted_iota(jnp.int32, (own, own), 0)
     ci = lax.broadcasted_iota(jnp.int32, (own, own), 1)
     to_patch_major = jnp.where(ci == lax.rem(ri, 2) * span + ri // 2, 1.0, 0.0).astype(BF16)
     for c in range(CHUNKS):
-        state = ownf[c]
-        for d in (1, 2, 3):
-            bulk_copy(c, d).wait_recv()
-            state = state + brecv[c, d - 1].astype(F32)
-        bst[c * own : (c + 1) * own] = dot(to_patch_major, state.astype(BF16)).astype(BF16)
+        for b in range(2):
+            bulk_up(c, b).wait_recv()
+            bulk_down(c, b).wait_recv()
+        state = jnp.concatenate(
+            [
+                ownf[c, b * span : (b + 1) * span] + brecv[c, 0, b].astype(F32) + brecv[c, 1, b].astype(F32)
+                for b in range(2)
+            ],
+            axis=0,
+        ).astype(BF16)
+        bst[c * own : (c + 1) * own] = dot(to_patch_major, state).astype(BF16)
 
     sources, blocks = owners_ref.shape
     spread = jnp.where(
@@ -427,10 +516,13 @@
 
     per = patches // plane
     loads[8].wait()
+    for b in range(2):
+        r_up(b).wait_recv()
+        r_down(b).wait_recv()
     total = update + pin[z].reshape(patches, piece).astype(F32)
-    for d in (1, 3, 2):
-        r_copy(d).wait_recv()
-        total = total + rrecv[d - 1].astype(F32)
+    total = total + jnp.concatenate(
+        [rrecv[0, b].astype(F32) + rrecv[1, b].astype(F32) for b in range(2)], axis=0
+    )
     result = total.astype(BF16)
     sorted_rows = dot(pick, result)
     for o in range(plane):
@@ -471,7 +563,8 @@
         for d in (1, 2, 3):
             pp_copy(c, d).wait_send()
             ag_copy(c, d).wait_send()
-            bulk_copy(c, d).wait_send()
+        for copy in (*bulk_far(c), bulk_up(c, 0), bulk_up(c, 1), bulk_down(c, 0), bulk_down(c, 1)):
+            copy.wait_send()
         return carry
 
     lax.fori_loop(0, CHUNKS, drain, 0)
@@ -479,8 +572,20 @@
         xk_copy(d).wait_send()
         xq_copy(d).wait_send()
         o_copy(d).wait_send()
-        r_copy(d).wait_send()
-    for copy in (own_up, own_down, relay_up, relay_down, *give):
+    for d in range(XN):
+        spread_piece(d, sent)
+
+    @pl.when(inner)
+    def _():
+        for d in (0, 2):
+            up_copy(y3, d, ru_s, ru_r).wait_send()
+
+    @pl.when(outer)
+    def _():
+        for d in (1, 3):
+            down_copy(y1, d, rd_s, rd_r).wait_send()
+
+    for copy in (q_give, o_give, st_give, far_up, far_down, r_up(0), r_up(1), r_down(0), r_down(1)):
         copy.wait_send()
 
 
@@ -512,8 +617,9 @@
         buf(rows, ff),
         buf(rows, dl, dtype=F32),
         buf(rows, gp, dtype=F32),
-        buf(CHUNKS, ZN, own, dl),
-        buf(CHUNKS, ZN - 1, own, dl),
+        buf(CHUNKS, ZN, 2, span, dl),
+        buf(CHUNKS, 2, span, dl),
+        buf(CHUNKS, 2, 2, span, dl),
         buf(CHUNKS, own, dl, dtype=F32),
         buf(CHUNKS, ZN, span, 2 * gp),
         buf(CHUNKS, ZN - 1, span, 2 * gp),
@@ -521,20 +627,27 @@
         buf(ZN, CHUNKS, span, piece),
         buf(patches, gw),
         buf(XN, 3, patches, HD),
-        buf(YN, 2, XN, 2, patches, HD),
-        buf(XN, patches, HD),
-        buf(XN, patches, 1, dtype=F32),
-        buf(XN, patches, 1, dtype=F32),
-        buf(XN, patches, HD, dtype=F32),
+        buf(YN, XN, 2, patches, HD),
+        buf(2, XN, patches, HD),
+        buf(2, 1, XN * patches, dtype=F32),
+        buf(2, 1, XN * patches, dtype=F32),
+        buf(2, HD, XN * patches, dtype=F32),
+        buf(HD, XN * patches),
+        buf(HD, XN * patches),
+        buf(8, XN * patches, dtype=F32),
+        buf(8, XN * patches, dtype=F32),
         buf(XN, patches, HD),
         buf(XN, patches, HD),
-        buf(ZN - 1, patches, piece),
-        buf(ZN - 1, patches, piece),
+        buf(2, patches // 2, piece),
+        buf(2, patches // 2, piece),
+        buf(2, 2, patches // 2, piece),
+        buf(2, 2, patches // 2, piece),
         buf(2 * patches, dl),
         buf(plane, patches // plane, piece),
         dma((9,)),
     ]
-    scratch += [dma((CHUNKS, 3))] * 6 + [dma((3,))] * 4 + [dma((4,))] * 2 + [dma((5,))] * 2 + [dma((3,))] * 4 + [dma((plane - 1,))] * 2
+    scratch += [dma((CHUNKS, 3))] * 4 + [dma((CHUNKS, 2))] * 2 + [dma((CHUNKS, 4))] * 2
+    scratch += [dma((3,))] * 4 + [dma((4,))] * 8 + [dma((3,))] * 4 + [dma((2,))] * 2 + [dma((4,))] * 2 + [dma((plane - 1,))] * 2
     byte_out, global_state = pl.pallas_call(
         kernel,
         out_shape=(

time: 93.1 us -> 71.7 us (0.77)
  Pallas kernels: 88.6 us -> 67.2 us
    pallas_call x1, Pallas kernels: 88.6 us -> 67.2 us  [on_device(): pl.pallas_call(kernel, out_shape=(jax.ShapeDtypeStruct((2 * patches, dl),...]
where the time goes in v3:
time: 71.7 us; the launch traced here: 71.4 us
  Pallas kernels  67.2 us (94%)
  local copies, waits for them, and re-layouts  3.63 us (5%)
    pallas_call x1, Pallas kernels, on_device(): pl.pallas_call(kernel, out_shape=(jax.ShapeDtypeStruct((2 * patches, dl),...  67.2 us
    reshape x1, local copies, waits for them, and re-layouts, on_device(): byte_out.reshape(patches, 2, dl)  2.03 us
    reshape x1, local copies, waits for them, and re-layouts, on_device(): global_state.reshape(patches, piece)  1.59 us

profile of v3, /device:TPU:1, one launch (start us, length us, event | category | flops | bytes accessed | tf_op | source)
XLA Modules:
  0.0 71.4 jit_solution(6266509284909324596)
XLA Ops:
  0.6 67.2 %shard_map.149 = (bf16[256,1024]{1,0:T(8,128)(2,1)}, bf16[32,4,512]{2,1,0:T(4,128)(2,1)}) custom-call(bf16[1024,1024]{1,0:T(8,128)(2,1)} %bitcast.6, bf16[3,1024,256]{2,1,0:T(8,128)(2,1)} %bitcast.7, bf16[256,1024]{1,0:T(8,128)(2,1)} %wo_hbm.1, bf16[1024,1024]{1,0:T(8,128)(2,1)} %up_hbm.1, bf16[1024,1024]{1,0:T(8,128)(2,1)} %down_hbm.1, ...), custom_call_target="tpu_custom_call" | custom-call | tf_op jit(solution)/shard_map/pallas_call | solution.py:651
  67.8 2.0 %reshape.22 = bf16[128,2,1024]{2,1,0:T(2,128)(2,1)} reshape(bf16[256,1024]{1,0:T(8,128)(2,1)} %get-tuple-element.4) | data formatting | bytes 1048576 | tf_op jit(solution)/shard_map/reshape | solution.py:664
  69.9 1.6 %reshape.23 = bf16[128,512]{1,0:T(8,128)(2,1)} reshape(bf16[32,4,512]{2,1,0:T(4,128)(2,1)} %get-tuple-element.5) | data formatting | bytes 262144 | tf_op jit(solution)/shard_map/reshape | solution.py:664

commit v4 on v3

v4 whole, which is shorter than its diff:
```python
import functools
import math

import jax
import jax.numpy as jnp
from jax import lax
from jax.experimental import pallas as pl
from jax.experimental.pallas import tpu as pltpu
from jax.sharding import PartitionSpec as P

EPS = 1e-06
NEG = -1e30
MESH = pl.DeviceIdType.MESH
F32 = jnp.float32
BF16 = jnp.bfloat16
XN = 4
YN = 4
ZN = 4
CHUNKS = 4
HD = 128


def dot(a, b):
    return jnp.dot(a, b, preferred_element_type=F32)


def dot_t(a, b):
    return lax.dot_general(a, b, (((1,), (1,)), ((), ())), preferred_element_type=F32)


def unit(v):
    return v * lax.rsqrt(jnp.mean(v * v, axis=-1, keepdims=True) + EPS)


def kernel(
    x_hbm, wqkv_hbm, wo_hbm, up_hbm, down_hbm, pp_hbm, gqkv_hbm, gout_hbm, back_hbm,
    gain_ref, ggain_ref, owners_ref, lscale_ref, gscale_ref,
    byte_hbm, state_ref,
    xv, wqkv, wo, up, down, ppw, gqkv, gout, back,
    xps, normed, act, part, ppf, bsend, bfar, brecv, ownf, ppsend, pprecv, ppown, pin,
    mixed_qkv, qkvs, kvbuf, qbuf, m_ref, l_ref, acc, opart, oget, stpart, stget, osend, orecv, rfar, rsend, rrecv, bst, psend, byte_ref,
    lsem, x_sem, pp_s, pp_r, ag_s, ag_r, bf_r, bk_s, bk_r, x_s, xk_r, xq_r,
    yu_s, yu_r, yd_s, yd_r, ru_s, ru_r, rd_s, rd_r, c_s, c_r, o_r, rf_r, r_s, r_r, p_s, p_r,
):
    s = lax.axis_index("seq")
    z = lax.axis_index("head")
    core = lax.rem(s, 2)
    x = lax.rem(s // 2, XN)
    y = s // (2 * XN)
    rows = xv.shape[0] // CHUNKS
    span = rows // 8
    own = 2 * span

    def seq_of(yy, xx, cc):
        return (yy * XN + xx) * 2 + cc

    def zpeer(d):
        return (s, lax.rem(z + d, ZN))

    def xpeer(d):
        return (seq_of(y, lax.rem(x + d, XN), core), z)

    y_up = (seq_of(lax.rem(y + 1, YN), x, core), z)
    y_down = (seq_of(lax.rem(y + YN - 1, YN), x, core), z)
    sibling = (seq_of(y, x, 1 - core), z)

    loads = [
        pltpu.make_async_copy(a, b, lsem.at[i])
        for i, (a, b) in enumerate(
            ((wqkv_hbm, wqkv), (up_hbm, up), (wo_hbm, wo), (down_hbm, down), (pp_hbm, ppw),
             (gqkv_hbm, gqkv), (gout_hbm, gout), (back_hbm, back))
        )
    ]
    def xload(c):
        at = pl.ds(pl.multiple_of(c * rows, rows), rows)
        return pltpu.make_async_copy(x_hbm.at[at], xv.at[at], x_sem.at[c])

    xload(0).start()
    loads[0].start()

    barrier = pltpu.get_barrier_semaphore()
    plane = 2 * XN * YN

    def greet(peer):
        pl.semaphore_signal(barrier, inc=1, device_id=peer, device_id_type=MESH)

    def greet_plane(d, carry):
        greet((lax.rem(s + d, plane), z))
        return carry

    for d in (1, 2, 3):
        greet(zpeer(d))
    lax.fori_loop(1, plane, greet_plane, 0)

    def remote(src, dst, ss, rs, peer):
        return pltpu.make_async_remote_copy(
            src_ref=src, dst_ref=dst, send_sem=ss, recv_sem=rs, device_id=peer, device_id_type=MESH
        )

    def pp_copy(c, d):
        return remote(
            ppsend.at[c, lax.rem(z + d, ZN)], pprecv.at[c, d - 1], pp_s.at[0], pp_r.at[c], zpeer(d)
        )

    def ag_copy(c, d):
        return remote(pin.at[z, c], pin.at[z, c], ag_s.at[0], ag_r.at[d - 1], zpeer(d))

    z_up = zpeer(1)
    z_down = zpeer(ZN - 1)
    up_at = lax.rem(z + 1, ZN)
    down_at = lax.rem(z + ZN - 1, ZN)
    far_at = lax.rem(z + 2, ZN)

    def bulk_far(c):
        return (
            remote(bsend.at[c, far_at, 0], bfar.at[c, 0], bk_s.at[0], bf_r.at[0], z_up),
            remote(bsend.at[c, far_at, 1], bfar.at[c, 1], bk_s.at[0], bf_r.at[0], z_down),
        )

    def bulk_up(c, b):
        return remote(bsend.at[c, up_at, b], brecv.at[c, 0, b], bk_s.at[0], bk_r.at[0], z_up)

    def bulk_down(c, b):
        return remote(bsend.at[c, down_at, b], brecv.at[c, 1, b], bk_s.at[0], bk_r.at[0], z_down)

    def bulk_combine(c, carry):
        bsend[c, up_at, 0] = (bsend[c, up_at, 0].astype(F32) + bfar[c, 0].astype(F32)).astype(BF16)
        bulk_up(c, 0).start()
        bsend[c, down_at, 1] = (bsend[c, down_at, 1].astype(F32) + bfar[c, 1].astype(F32)).astype(BF16)
        bulk_down(c, 1).start()
        return carry

    def arrived(ref, sem):
        pltpu.make_async_copy(ref, ref, sem).wait()

    def finish_patches(c):
        total = ppown[c]
        arrived(pprecv.at[c], pp_r.at[c])
        for d in (1, 2, 3):
            total = total + pprecv[c, d - 1].astype(F32)
        pin[z, c] = total.astype(BF16)
        for d in (2, 1, 3):
            ag_copy(c, d).start()

    row_i = lax.broadcasted_iota(jnp.int32, (rows, rows), 0)
    col_i = lax.broadcasted_iota(jnp.int32, (rows, rows), 1)
    to_byte_major = jnp.where(
        col_i == lax.rem(row_i, span) * 8 + row_i // span, 1.0, 0.0
    ).astype(BF16)

    def prepare(c, slot):
        xp = dot(to_byte_major, xv[pl.ds(pl.multiple_of(c * rows, rows), rows), :])
        xps[slot] = xp.astype(BF16)
        normed[slot] = (
            xp * lax.rsqrt(jnp.mean(xp * xp, axis=-1, keepdims=True) + EPS) * gain_ref[...]
        ).astype(BF16)

    def gelu(v):
        inner = v * (0.7978845608028654 + (0.7978845608028654 * 0.044715) * (v * v))
        half = 0.5 * v
        return (half + half * jnp.tanh(inner)).astype(BF16)

    rr = lax.broadcasted_iota(jnp.int32, (rows, rows), 0)
    cc = lax.broadcasted_iota(jnp.int32, (rows, rows), 1)
    seen = (lax.rem(rr, span) == lax.rem(cc, span)) & (cc // span <= rr // span)

    def chunk(c, ahead):
        slot = lax.rem(c, 2)
        nv = normed[slot]
        tiles = [slice(n * 256, (n + 1) * 256) for n in range(up.shape[1] // 256)]
        cuts = [slice(h * HD, (h + 1) * HD) for h in range(2)]
        q2 = dot(nv, wqkv[0])
        k2 = dot(nv, wqkv[1])
        v2 = dot(nv, wqkv[2]).astype(BF16)
        hidden = dot(nv, up[:, tiles[0]])
        qs = [unit(q2[:, cut]).astype(BF16) for cut in cuts]
        ks = [unit(k2[:, cut]).astype(BF16) for cut in cuts]
        later = dot(nv, up[:, tiles[1]])
        scores = [dot_t(qs[h], ks[h]) for h in range(2)]
        act[:, tiles[0]] = gelu(hidden)
        hidden = dot(nv, up[:, tiles[2]])
        es, totals = [], []
        for h in range(2):
            sc = jnp.where(seen, scores[h] * (lscale_ref[h] / math.sqrt(HD)), NEG)
            e = jnp.exp(sc - jnp.max(sc, axis=-1, keepdims=True))
            totals.append(jnp.sum(e, axis=-1, keepdims=True))
            es.append(e.astype(BF16))
        act[:, tiles[1]] = gelu(later)
        later = dot(nv, up[:, tiles[3]])
        heads = [(dot(es[h], v2[:, cuts[h]]) / totals[h]).astype(BF16) for h in range(2)]
        lo = jnp.concatenate(heads, axis=1)
        act[:, tiles[2]] = gelu(hidden)
        act[:, tiles[3]] = gelu(later)
        if ahead is not None:
            xload(ahead).wait()
            prepare(ahead, 1 - slot)
        mine = lax.broadcasted_iota(jnp.int32, (rows, 1), 0) // own == z
        a = act[...]
        for cut in tiles:
            t = dot(lo, wo[:, cut]) + dot(a, down[:, cut])
            t = t + jnp.where(mine, xps[slot, :, cut].astype(F32), 0.0)
            part[:, cut] = t
            tb = t.astype(BF16)
            for h in range(ZN):
                for b in range(2):
                    at = h * own + b * span
                    bsend[c, h, b, :, cut] = tb[at : at + span]
        ownf[c] = part[pl.ds(pl.multiple_of(z * own, own), own), :]
        pp = dot(bsend[c].reshape(rows, part.shape[1]), ppw[...])
        ppf[...] = pp
        pb = pp.astype(BF16)
        gp = pp.shape[1]
        for h in range(ZN):
            for b in range(2):
                at = (2 * h + b) * span
                ppsend[c, h, :, b * gp : (b + 1) * gp] = pb[at : at + span]
        for b in range(2):
            at = pl.multiple_of(z * own + b * span, span)
            ppown[c, :, b * gp : (b + 1) * gp] = ppf[pl.ds(at, span), :]

        @pl.when(c == 0)
        def _():
            pl.semaphore_wait(barrier, ZN - 1 + plane - 1)

        for d in (2, 1, 3):
            pp_copy(c, d).start()

        @pl.when(c >= 1)
        def _():
            finish_patches(c - 1)


    xload(0).wait()
    for load in loads[1:4]:
        load.start()
    for c in range(1, CHUNKS):
        xload(c).start()
    for load in loads[4:]:
        load.start()
    prepare(jnp.int32(0), 0)
    for load in loads[:5]:
        load.wait()

    def chunk_step(c, carry):
        chunk(c, c + 1)
        return carry

    lax.fori_loop(0, CHUNKS - 1, chunk_step, 0)
    chunk(jnp.int32(CHUNKS - 1), None)
    finish_patches(CHUNKS - 1)
    loads[5].wait()
    patches = CHUNKS * span
    piece = pin.shape[3]
    square = jnp.zeros((patches, 1), F32)
    for d in (0, 1, 3, 2):
        h = lax.rem(z + ZN - d, ZN)
        if d:
            arrived(pin.at[h], ag_r.at[d - 1])
        if d == 2:
            for c in range(CHUNKS):
                for copy in bulk_far(c):
                    copy.start()
            for c in range(CHUNKS):
                bulk_up(c, 1).start()
                bulk_down(c, 0).start()
        at = pl.ds(pl.multiple_of(h * piece, piece), piece)
        v = pin[h].reshape(patches, piece).astype(F32)
        square = square + jnp.sum(v * v, axis=-1, keepdims=True)
        g = (v * ggain_ref[:, at]).astype(BF16)
        for j in (1, 2, 0):
            for half in range(2):
                cut = slice(half * 256, (half + 1) * 256)
                r = dot(g, gqkv[j, at, cut])
                mixed_qkv[j, :, cut] = r if d == 0 else mixed_qkv[j, :, cut] + r
    inv = lax.rsqrt(square / (ZN * piece) + EPS)

    def project(j):
        for t in range(XN):
            v = mixed_qkv[j, :, t * HD : (t + 1) * HD] * inv
            if j < 2:
                v = unit(v)
            if j == 2:
                v = jnp.transpose(v)
            qkvs[t, j] = v.astype(BF16)

    def xk_copy(d):
        h = lax.rem(x + d, XN)
        return remote(qkvs.at[h, pl.ds(1, 2)], kvbuf.at[y, x], x_s.at[0], xk_r.at[d - 1], xpeer(d))

    def src(d):
        return lax.rem(x + XN - d, XN)

    def xk_arrival(d):
        at = kvbuf.at[y, src(d)]
        return pltpu.make_async_copy(at, at, xk_r.at[d - 1])

    def xq_copy(d):
        h = lax.rem(x + d, XN)
        return remote(qkvs.at[h, 0], qbuf.at[0, x], x_s.at[0], xq_r.at[0], xpeer(d))

    y1 = lax.rem(y + 1, YN)
    y2 = lax.rem(y + 2, YN)
    y3 = lax.rem(y + 3, YN)

    def up_copy(row, d, ss, rs):
        at = kvbuf.at[row, src(d)]
        return remote(at, at, ss.at[d], rs.at[d], y_up)

    def down_copy(row, d, ss, rs):
        at = kvbuf.at[row, src(d)]
        return remote(at, at, ss.at[d], rs.at[d], y_down)

    def relay_up(row, d):
        at = kvbuf.at[row, src(d)]
        return remote(at, at, ru_s.at[d // 2], ru_r.at[d // 2], y_up)

    def relay_down(row, d):
        at = kvbuf.at[row, src(d)]
        return remote(at, at, rd_s.at[d // 2], rd_r.at[d // 2], y_down)

    last = YN - 1
    inner = (y >= 1) & (y < last)
    outer = (y == 0) | (y == last)

    def spread_piece(d, act_on):
        @pl.when(y < last)
        def _():
            act_on(up_copy(y, d, yu_s, yu_r))

        @pl.when((y == 0) | ((y == 1) & (d % 2 == 1)))
        def _():
            act_on(down_copy(y, d, yd_s, yd_r))

    def start(copy):
        copy.start()

    def sent(copy):
        copy.wait_send()

    def take_down(d):
        @pl.when(y >= 1)
        def _():
            up_copy(y3, d, yu_s, yu_r).wait_recv()

        if d % 2 == 0:

            @pl.when(inner)
            def _():
                relay_up(y3, d).start()

    def take_up(d):
        @pl.when((y == last) | ((y == 0) & (d % 2 == 1)))
        def _():
            down_copy(y1, d, yd_s, yd_r).wait_recv()

        if d % 2 == 1:

            @pl.when(outer)
            def _():
                relay_down(y1, d).start()

    def take_far():
        @pl.when(y >= 2)
        def _():
            for d in (0, 2):
                relay_up(y2, d).wait_recv()
            for d in (1, 3):
                relay_down(y2, d).wait_recv()

    q_give = remote(qbuf.at[0], qbuf.at[1], c_s.at[0], c_r.at[0], sibling)
    o_give = remote(opart, oget, c_s.at[1], c_r.at[1], sibling)
    st_give = remote(stpart, stget, c_s.at[2], c_r.at[2], sibling)

    project(1)
    project(2)
    for d in (2, 1, 3):
        xk_copy(d).start()
    kvbuf[y, x] = qkvs[x, 1:3]
    spread_piece(0, start)
    project(0)
    for d in (2, 1, 3):
        xq_copy(d).start()
    qbuf[0, x] = qkvs[x, 0]
    m_ref[...] = jnp.full(m_ref.shape, NEG, F32)
    l_ref[...] = jnp.zeros(l_ref.shape, F32)
    acc[...] = jnp.zeros(acc.shape, F32)
    factor = gscale_ref[x] * (math.log2(math.e) / math.sqrt(HD))

    for d in (3, 1, 2):
        xk_arrival(d).wait()
        spread_piece(d, start)
    arrived(qbuf.at[0, pl.ds(0, XN - 1)], xq_r.at[0])
    q_give.start()

    half_q = XN * patches // 2

    def attend(yb, rels, masked):
        chains = [(rel, part_q) for rel in rels for part_q in range(2)]

        def raw(chain):
            rel, part_q = chain
            wide = (part_q + 1) * XN // 2 if masked else XN
            queries = qbuf[rel].reshape(XN * patches, HD)[part_q * half_q : (part_q + 1) * half_q]
            scores = dot_t(kvbuf[yb, 0:wide, 0].reshape(wide * patches, HD), queries)
            if masked:
                kk = lax.broadcasted_iota(jnp.int32, scores.shape, 0)
                qq = lax.broadcasted_iota(jnp.int32, scores.shape, 1) + part_q * half_q
                theirs = core + rel * (1 - 2 * core)
                k_at = kk + (kk // patches + core) * patches
                q_at = qq + (qq // patches + theirs) * patches
                scores = jnp.where(k_at <= q_at, scores, NEG)
            return scores

        def fold(op, v):
            return op(op(v.reshape(8, v.shape[0] // 8, v.shape[1]), axis=0), axis=0, keepdims=True)

        upcoming = raw(chains[0])
        for i, (rel, part_q) in enumerate(chains):
            scores = upcoming
            if i + 1 < len(chains):
                upcoming = raw(chains[i + 1])
            cut = slice(part_q * half_q, (part_q + 1) * half_q)
            old = m_ref[rel, :, cut]
            new = jnp.maximum(old, fold(jnp.max, scores))
            keep = jnp.exp2((old - new) * factor)
            e = jnp.exp2((scores - new) * factor)
            m_ref[rel, :, cut] = new
            l_ref[rel, :, cut] = l_ref[rel, :, cut] * keep + fold(jnp.sum, e)
            wide = scores.shape[0] // patches
            vt = jnp.concatenate([kvbuf[yb, k, 1] for k in range(wide)], axis=1)
            acc[rel, :, cut] = acc[rel, :, cut] * keep + dot(vt, e.astype(BF16))

    def run(yb, rels):
        @pl.when(yb < y)
        def _():
            attend(yb, rels, False)


    attend(y, (0,), True)
    take_down(0)
    take_up(0)
    q_give.wait_recv()
    attend(y, (1,), True)
    for d in (3, 1, 2):
        take_up(d)
        take_down(d)
    run(y3, (1, 0))
    run(y1, (1, 0))
    arrived(bfar, bf_r.at[0])
    lax.fori_loop(0, CHUNKS, bulk_combine, 0)
    take_far()
    run(y2, (1,))
    opart[...] = (acc[1] / l_ref[1]).astype(BF16)
    stpart[...] = jnp.zeros(stpart.shape, F32)
    stpart[0:1] = m_ref[1]
    stpart[1:2] = l_ref[1]
    o_give.start()
    st_give.start()
    run(y2, (0,))
    o_give.wait_recv()
    st_give.wait_recv()
    m0, m1 = m_ref[0], stget[0:1]
    top = jnp.maximum(m0, m1)
    w0 = jnp.exp2((m0 - top) * factor)
    w1 = jnp.exp2((m1 - top) * factor) * stget[1:2]
    mixed = (acc[0] * w0 + oget[...].astype(F32) * w1) / (l_ref[0] * w0 + w1)
    for qb in range(XN):
        osend[qb] = jnp.transpose(mixed[:, qb * patches : (qb + 1) * patches]).astype(BF16)

    def o_copy(d):
        h = lax.rem(x + d, XN)
        return remote(osend.at[h], orecv.at[x], x_s.at[0], o_r.at[0], xpeer(d))

    for d in (2, 1, 3):
        o_copy(d).start()
    orecv[x] = osend[x]
    loads[6].wait()
    arrived(orecv.at[pl.ds(0, XN - 1)], o_r.at[0])
    gattn = jnp.concatenate([orecv[h] for h in range(XN)], axis=1)

    def out_part(zz):
        return dot(gattn, gout[:, pl.ds(pl.multiple_of(zz * piece, piece), piece)])

    half_p = patches // 2
    low, high = slice(0, half_p), slice(half_p, patches)
    far_up = remote(rsend.at[2, 0], rfar.at[0], r_s.at[0], rf_r.at[0], z_up)
    far_down = remote(rsend.at[2, 1], rfar.at[1], r_s.at[0], rf_r.at[1], z_down)

    def r_up(b):
        return remote(rsend.at[0, b], rrecv.at[0, b], r_s.at[0], r_r.at[0], z_up)

    def r_down(b):
        return remote(rsend.at[1, b], rrecv.at[1, b], r_s.at[0], r_r.at[0], z_down)

    far_part = out_part(far_at).astype(BF16)
    rsend[2, 0] = far_part[low]
    far_up.start()
    rsend[2, 1] = far_part[high]
    far_down.start()
    up_part = out_part(up_at)
    rsend[0, 1] = up_part[high].astype(BF16)
    down_part = out_part(down_at)
    rsend[1, 0] = down_part[low].astype(BF16)
    update = out_part(z)

    ri = lax.broadcasted_iota(jnp.int32, (own, own), 0)
    ci = lax.broadcasted_iota(jnp.int32, (own, own), 1)
    to_patch_major = jnp.where(ci == lax.rem(ri, 2) * span + ri // 2, 1.0, 0.0).astype(BF16)
    arrived(brecv, bk_r.at[0])
    for c in range(CHUNKS):
        state = jnp.concatenate(
            [
                ownf[c, b * span : (b + 1) * span] + brecv[c, 0, b].astype(F32) + brecv[c, 1, b].astype(F32)
                for b in range(2)
            ],
            axis=0,
        ).astype(BF16)
        bst[c * own : (c + 1) * own] = dot(to_patch_major, state).astype(BF16)

    r_up(1).start()
    r_down(0).start()
    sources, blocks = owners_ref.shape
    spread = jnp.where(
        lax.broadcasted_iota(jnp.int32, (blocks, patches), 1) // 2
        == lax.broadcasted_iota(jnp.int32, (blocks, patches), 0),
        1.0,
        0.0,
    ).astype(BF16)
    listed = dot(owners_ref[...].astype(F32).astype(BF16), spread)
    is_mine = lax.broadcasted_iota(jnp.int32, listed.shape, 0) == s
    listed_row = jnp.sum(jnp.where(is_mine, listed, 0.0), axis=0, keepdims=True)
    pr = lax.broadcasted_iota(jnp.int32, (patches, patches), 0)
    pc = lax.broadcasted_iota(jnp.int32, (patches, patches), 1)
    listed_col = jnp.sum(jnp.where(pr == pc, listed_row, 0.0), axis=1, keepdims=True)
    earlier = (listed_col == listed_row) & (pr < pc) & (lax.rem(pr, 2) == lax.rem(pc, 2))
    rank = jnp.sum(jnp.where(earlier, 1.0, 0.0), axis=0, keepdims=True)
    slot = listed_row * 4.0 + rank * 2.0 + lax.rem(pc, 2).astype(F32)
    pick = jnp.where(slot == pr.astype(F32), 1.0, 0.0).astype(BF16)

    per = patches // plane
    loads[7].wait()
    far_up.wait_recv()
    rsend[0, 0] = (up_part[low] + rfar[0].astype(F32)).astype(BF16)
    r_up(0).start()
    far_down.wait_recv()
    rsend[1, 1] = (down_part[high] + rfar[1].astype(F32)).astype(BF16)
    r_down(1).start()
    arrived(rrecv, r_r.at[0])
    total = update + pin[z].reshape(patches, piece).astype(F32)
    total = total + jnp.concatenate(
        [rrecv[0, b].astype(F32) + rrecv[1, b].astype(F32) for b in range(2)], axis=0
    )
    result = total.astype(BF16)
    sorted_rows = dot(pick, result)
    for o in range(plane):
        psend[o] = sorted_rows[o * per : (o + 1) * per].astype(BF16)

    def p_copy(d):
        return remote(
            psend.at[lax.rem(s + d, plane)], state_ref.at[s], p_s.at[0], p_r.at[0], (lax.rem(s + d, plane), z)
        )

    def p_start(d, carry):
        p_copy(d).start()
        return carry

    lax.fori_loop(1, plane, p_start, 0)
    keep_own = pltpu.make_async_copy(psend.at[s], state_ref.at[s], lsem.at[9])
    keep_own.start()
    gp = back.shape[0]
    re = lax.broadcasted_iota(jnp.int32, (2 * patches, patches), 0)
    ce = lax.broadcasted_iota(jnp.int32, (2 * patches, patches), 1)
    shares = jnp.zeros((2 * patches, gp), F32)
    for b in range(2):
        lift = jnp.where(re == 2 * ce + b, 1.0, 0.0).astype(BF16)
        shares = shares + dot(lift, result[:, b * gp : (b + 1) * gp])
    shares = shares.astype(BF16)
    for n in range(bst.shape[1] // 256):
        cut = slice(n * 256, (n + 1) * 256)
        both = bst[:, cut].astype(F32) + dot(shares, back[:, cut])
        byte_ref[:, :, cut] = both.astype(BF16).reshape(patches, 2, 256)

    byte_put = pltpu.make_async_copy(byte_ref, byte_hbm, lsem.at[8])
    byte_put.start()
    arrived(state_ref.at[pl.ds(0, plane - 1)], p_r.at[0])

    byte_put.wait()
    keep_own.wait()
    arrived(psend.at[pl.ds(0, plane - 1)], p_s.at[0])
    arrived(ppsend.at[pl.ds(0, ZN - 1)], pp_s.at[0])
    arrived(pin.at[pl.ds(0, ZN - 1)], ag_s.at[0])
    arrived(bsend.at[pl.ds(0, ZN - 1)], bk_s.at[0])
    arrived(qkvs, x_s.at[0])
    arrived(rsend, r_s.at[0])
    for d in range(XN):
        spread_piece(d, sent)

    @pl.when(inner)
    def _():
        for d in (0, 2):
            relay_up(y3, d).wait_send()

    @pl.when(outer)
    def _():
        for d in (1, 3):
            relay_down(y1, d).wait_send()

    for copy in (q_give, o_give, st_give):
        copy.wait_send()


def settle(a_hbm, b_hbm, a_out, b_out, va, vb, wb, in_sem, out_sem):
    cut = va.shape[0] // 4
    takes, puts = [], []
    for i in range(4):
        at = pl.ds(i * cut, cut)
        takes.append(pltpu.make_async_copy(a_hbm.at[at], va.at[at], in_sem.at[i]))
        puts.append(pltpu.make_async_copy(va.at[at], a_out.at[at], out_sem.at[i]))
    last = pltpu.make_async_copy(b_hbm, vb, in_sem.at[4])
    put_last = pltpu.make_async_copy(wb, b_out, out_sem.at[4])
    last.start()
    for take in takes:
        take.start()
    last.wait()
    wb[...] = jnp.concatenate([vb[o].astype(F32) for o in range(vb.shape[0])], axis=0).astype(BF16)
    put_last.start()
    for take, put in zip(takes, puts):
        take.wait()
        put.start()
    for put in puts:
        put.wait()
    put_last.wait()


def on_device(
    byte_in, local_gain, local_qkv, local_out, mlp_up, mlp_down, local_scale, patch_proj,
    global_gain, global_qkv, global_out, global_scale, back_proj, owners,
):
    patches, span8, dl = byte_in.shape
    gw = global_out.shape[1]
    piece = gw // ZN
    ff = mlp_up.shape[1]
    rows = patches * span8 // CHUNKS
    span = patches // CHUNKS
    own = 2 * span
    gp = back_proj.shape[0]
    plane = 2 * XN * YN
    wqkv3 = jnp.transpose(local_qkv, (1, 0, 2))
    gqkv3 = jnp.transpose(global_qkv, (1, 0, 2))
    hbm = pl.BlockSpec(memory_space=pl.ANY)
    vm = pl.BlockSpec(memory_space=pltpu.VMEM)
    sm = pl.BlockSpec(memory_space=pltpu.SMEM)
    dma = pltpu.SemaphoreType.DMA

    def buf(*shape, dtype=BF16):
        return pltpu.VMEM(shape, dtype)

    big = [byte_in.reshape(patches * span8, dl), wqkv3, local_out, mlp_up, mlp_down, patch_proj, gqkv3, global_out, back_proj]
    scratch = [buf(*a.shape) for a in big] + [
        buf(2, rows, dl),
        buf(2, rows, dl),
        buf(rows, ff),
        buf(rows, dl, dtype=F32),
        buf(rows, gp, dtype=F32),
        buf(CHUNKS, ZN, 2, span, dl),
        buf(CHUNKS, 2, span, dl),
        buf(CHUNKS, 2, 2, span, dl),
        buf(CHUNKS, own, dl, dtype=F32),
        buf(CHUNKS, ZN, span, 2 * gp),
        buf(CHUNKS, ZN - 1, span, 2 * gp),
        buf(CHUNKS, span, 2 * gp, dtype=F32),
        buf(ZN, CHUNKS, span, piece),
        buf(3, patches, piece, dtype=F32),
        buf(XN, 3, patches, HD),
        buf(YN, XN, 2, patches, HD),
        buf(2, XN, patches, HD),
        buf(2, 1, XN * patches, dtype=F32),
        buf(2, 1, XN * patches, dtype=F32),
        buf(2, HD, XN * patches, dtype=F32),
        buf(HD, XN * patches),
        buf(HD, XN * patches),
        buf(8, XN * patches, dtype=F32),
        buf(8, XN * patches, dtype=F32),
        buf(XN, patches, HD),
        buf(XN, patches, HD),
        buf(2, patches // 2, piece),
        buf(3, 2, patches // 2, piece),
        buf(2, 2, patches // 2, piece),
        buf(2 * patches, dl),
        buf(plane, patches // plane, piece),
        buf(patches, 2, dl),
        dma((10,)),
        dma((CHUNKS,)),
    ]
    counts = (1, CHUNKS, 1, 3, 1, 1, 1, 1, 3, 1, 4, 4, 4, 4, 2, 2, 2, 2, 3, 3, 1, 2, 1, 1, 1, 1)
    scratch += [dma((n,)) for n in counts]
    byte_out, global_state = pl.pallas_call(
        kernel,
        out_shape=(
            jax.ShapeDtypeStruct((patches, 2, dl), BF16),
            jax.ShapeDtypeStruct((plane, patches // plane, piece), BF16),
        ),
        in_specs=[hbm] * 9 + [vm] * 3 + [sm] * 2,
        out_specs=(hbm, hbm),
        scratch_shapes=scratch,
        compiler_params=pltpu.CompilerParams(
            collective_id=0, has_side_effects=True, vmem_limit_bytes=60 * 1024 * 1024
        ),
    )(*big, local_gain.reshape(1, dl), global_gain.reshape(1, gw), owners, local_scale, global_scale)
    return pl.pallas_call(
        settle,
        out_shape=(
            jax.ShapeDtypeStruct(byte_out.shape, BF16),
            jax.ShapeDtypeStruct((patches, piece), BF16),
        ),
        in_specs=[hbm] * 2,
        out_specs=(hbm, hbm),
        scratch_shapes=[buf(*byte_out.shape), buf(*global_state.shape), buf(patches, piece), dma((5,)), dma((5,))],
    )(byte_out, global_state)


def solution(mesh):
    placed = (
        P("seq", None, None),
        P(),
        P(None, None, "head"),
        P("head", None),
        P(None, "head"),
        P("head", None),
        P("head"),
        P(),
        P(),
        P(None, None, "head"),
        P("head", None),
        P("head"),
        P(),
        P(),
    )
    return jax.shard_map(
        on_device,
        mesh=mesh,
        in_specs=placed,
        out_specs=(P("seq", "head", None), P("seq", "head")),
        check_vma=False,
    )
```

time: 71.7 us -> 66.6 us (0.929)
  local copies, waits for them, and re-layouts: 3.63 us -> 0 us
  Pallas kernels: 67.2 us -> 65.8 us
    reshape x2 -> x0, local copies, waits for them, and re-layouts: 3.63 us -> none  [the longest x1 2.03 us: on_device(): byte_out.reshape(patches, 2, dl)]
    pallas_call x1 -> x2, Pallas kernels: 67.2 us -> 65.8 us  [the longest x1 63.9 us: on_device(): pl.pallas_call(kernel, out_shape=(jax.ShapeDtypeStruct((patches, 2, dl),...]
where the time goes in v4:
time: 66.6 us; the launch traced here: 66.4 us
  Pallas kernels  65.8 us (99%)
    pallas_call x1, Pallas kernels, on_device(): pl.pallas_call(kernel, out_shape=(jax.ShapeDtypeStruct((patches, 2, dl),...  63.9 us
    pallas_call x1, Pallas kernels, on_device(): pl.pallas_call(settle, out_shape=(jax.ShapeDtypeStruct(byte_out.shape, BF...  1.91 us

profile of v4, /device:TPU:1, one launch (start us, length us, event | category | flops | bytes accessed | tf_op | source)
XLA Modules:
  0.0 66.4 jit_solution(8206495882450030758)
XLA Ops:
  0.6 63.9 %shard_map.149 = (bf16[128,2,1024]{2,1,0:T(2,128)(2,1)}, bf16[32,4,512]{2,1,0:T(4,128)(2,1)}) custom-call(bf16[1024,1024]{1,0:T(8,128)(2,1)} %bitcast.6, bf16[3,1024,256]{2,1,0:T(8,128)(2,1)} %bitcast.7, bf16[256,1024]{1,0:T(8,128)(2,1)} %wo_hbm.1, bf16[1024,1024]{1,0:T(8,128)(2,1)} %up_hbm.1, bf16[1024,1024]{1,0:T(8,128)(2,1)} %down_hbm.1, ...), custom_call_target="tpu_custom_call" | custom-call | tf_op jit(solution)/shard_map/pallas_call | solution.py:697
  64.5 1.9 %shard_map.150 = (bf16[128,2,1024]{2,1,0:T(2,128)(2,1)}, bf16[128,512]{1,0:T(8,128)(2,1)}) custom-call(bf16[128,2,1024]{2,1,0:T(2,128)(2,1)} %get-tuple-element.4.a_hbm, bf16[32,4,512]{2,1,0:T(4,128)(2,1)} %get-tuple-element.5.b_hbm), custom_call_target="tpu_custom_call" | custom-call | tf_op jit(solution)/shard_map/pallas_call | solution.py:710

commit v5 on v4

--- a/solution.py
+++ b/solution.py
@@ -39,7 +39,7 @@
     xv, wqkv, wo, up, down, ppw, gqkv, gout, back,
     xps, normed, act, part, ppf, bsend, bfar, brecv, ownf, ppsend, pprecv, ppown, pin,
     mixed_qkv, qkvs, kvbuf, qbuf, m_ref, l_ref, acc, opart, oget, stpart, stget, osend, orecv, rfar, rsend, rrecv, bst, psend, byte_ref,
-    lsem, x_sem, pp_s, pp_r, ag_s, ag_r, bf_r, bk_s, bk_r, x_s, xk_r, xq_r,
+    lsem, x_sem, pp_s, pp_r, ag_s, ag_r, an_r, bf_r, bk_s, bk_r, x_s, xk_r, xq_r,
     yu_s, yu_r, yd_s, yd_r, ru_s, ru_r, rd_s, rd_r, c_s, c_r, o_r, rf_r, r_s, r_r, p_s, p_r,
 ):
     s = lax.axis_index("seq")
@@ -76,7 +76,10 @@
         return pltpu.make_async_copy(x_hbm.at[at], xv.at[at], x_sem.at[c])
 
     xload(0).start()
-    loads[0].start()
+    for load in loads[:5]:
+        load.start()
+    for c in range(1, CHUNKS):
+        xload(c).start()
 
     barrier = pltpu.get_barrier_semaphore()
     plane = 2 * XN * YN
@@ -103,7 +106,13 @@
         )
 
     def ag_copy(c, d):
-        return remote(pin.at[z, c], pin.at[z, c], ag_s.at[0], ag_r.at[d - 1], zpeer(d))
+        rs = an_r.at[c] if d == ZN - 1 else ag_r.at[d - 1]
+        return remote(pin.at[z, c], pin.at[z, c], ag_s.at[0], rs, zpeer(d))
+
+    def ag_relay(c):
+        at = pin.at[up_at, c]
+        arrived(at, an_r.at[c])
+        remote(at, at, ag_s.at[0], ag_r.at[1], z_down).start()
 
     z_up = zpeer(1)
     z_down = zpeer(ZN - 1)
@@ -133,13 +142,13 @@
     def arrived(ref, sem):
         pltpu.make_async_copy(ref, ref, sem).wait()
 
-    def finish_patches(c):
+    def finish_patches(c, last_one=False):
         total = ppown[c]
         arrived(pprecv.at[c], pp_r.at[c])
         for d in (1, 2, 3):
             total = total + pprecv[c, d - 1].astype(F32)
         pin[z, c] = total.astype(BF16)
-        for d in (2, 1, 3):
+        for d in (2, 1, 3) if last_one else (1, 3):
             ag_copy(c, d).start()
 
     row_i = lax.broadcasted_iota(jnp.int32, (rows, rows), 0)
@@ -164,7 +173,7 @@
     cc = lax.broadcasted_iota(jnp.int32, (rows, rows), 1)
     seen = (lax.rem(rr, span) == lax.rem(cc, span)) & (cc // span <= rr // span)
 
-    def chunk(c, ahead):
+    def chunk(c, ahead, first=False):
         slot = lax.rem(c, 2)
         nv = normed[slot]
         tiles = [slice(n * 256, (n + 1) * 256) for n in range(up.shape[1] // 256)]
@@ -194,6 +203,11 @@
         if ahead is not None:
             xload(ahead).wait()
             prepare(ahead, 1 - slot)
+        if first:
+            for load in loads[2:5]:
+                load.wait()
+            for load in loads[5:]:
+                load.start()
         mine = lax.broadcasted_iota(jnp.int32, (rows, 1), 0) // own == z
         a = act[...]
         for cut in tiles:
@@ -229,25 +243,25 @@
         def _():
             finish_patches(c - 1)
 
+        @pl.when(c >= 2)
+        def _():
+            ag_relay(c - 2)
+
 
     xload(0).wait()
-    for load in loads[1:4]:
-        load.start()
-    for c in range(1, CHUNKS):
-        xload(c).start()
-    for load in loads[4:]:
-        load.start()
     prepare(jnp.int32(0), 0)
-    for load in loads[:5]:
+    for load in loads[:2]:
         load.wait()
 
     def chunk_step(c, carry):
         chunk(c, c + 1)
         return carry
 
-    lax.fori_loop(0, CHUNKS - 1, chunk_step, 0)
+    chunk(jnp.int32(0), jnp.int32(1), True)
+    lax.fori_loop(1, CHUNKS - 1, chunk_step, 0)
     chunk(jnp.int32(CHUNKS - 1), None)
-    finish_patches(CHUNKS - 1)
+    finish_patches(CHUNKS - 1, True)
+    ag_relay(CHUNKS - 2)
     loads[5].wait()
     patches = CHUNKS * span
     piece = pin.shape[3]
@@ -255,7 +269,10 @@
     for d in (0, 1, 3, 2):
         h = lax.rem(z + ZN - d, ZN)
         if d:
-            arrived(pin.at[h], ag_r.at[d - 1])
+            if d == ZN - 1:
+                arrived(pin.at[h, CHUNKS - 1], an_r.at[CHUNKS - 1])
+            else:
+                arrived(pin.at[h], ag_r.at[d - 1])
         if d == 2:
             for c in range(CHUNKS):
                 for copy in bulk_far(c):
@@ -555,16 +572,14 @@
     for o in range(plane):
         psend[o] = sorted_rows[o * per : (o + 1) * per].astype(BF16)
 
-    def p_copy(d):
-        return remote(
-            psend.at[lax.rem(s + d, plane)], state_ref.at[s], p_s.at[0], p_r.at[0], (lax.rem(s + d, plane), z)
-        )
-
-    def p_start(d, carry):
-        p_copy(d).start()
-        return carry
-
-    lax.fori_loop(1, plane, p_start, 0)
+    def p_copy(dy, dx, dc):
+        to = seq_of(lax.rem(y + dy, YN), lax.rem(x + dx, XN), lax.rem(core + dc, 2))
+        return remote(psend.at[to], state_ref.at[s], p_s.at[0], p_r.at[0], (to, z))
+
+    hops = [0, 1, 2, 1]
+    turns = [(dy, dx, dc) for dy in range(YN) for dx in range(XN) for dc in range(2) if dy or dx or dc]
+    for dy, dx, dc in sorted(turns, key=lambda turn: -hops[turn[0]] - hops[turn[1]]):
+        p_copy(dy, dx, dc).start()
     keep_own = pltpu.make_async_copy(psend.at[s], state_ref.at[s], lsem.at[9])
     keep_own.start()
     gp = back.shape[0]
@@ -692,7 +707,7 @@
         dma((10,)),
         dma((CHUNKS,)),
     ]
-    counts = (1, CHUNKS, 1, 3, 1, 1, 1, 1, 3, 1, 4, 4, 4, 4, 2, 2, 2, 2, 3, 3, 1, 2, 1, 1, 1, 1)
+    counts = (1, CHUNKS, 1, 3, CHUNKS, 1, 1, 1, 1, 3, 1, 4, 4, 4, 4, 2, 2, 2, 2, 3, 3, 1, 2, 1, 1, 1, 1)
     scratch += [dma((n,)) for n in counts]
     byte_out, global_state = pl.pallas_call(
         kernel,

time: 66.6 us -> 64.7 us (0.971)
  Pallas kernels: 65.8 us -> 63.7 us
    pallas_call x1, Pallas kernels: 63.9 us -> 61.8 us  [on_device(): pl.pallas_call(kernel, out_shape=(jax.ShapeDtypeStruct((patches, 2, dl),...]
where the time goes in v5:
time: 64.7 us; the launch traced here: 64.5 us
  Pallas kernels  63.7 us (98%)
  between operations  0.8 us (1%)
    pallas_call x1, Pallas kernels, on_device(): pl.pallas_call(kernel, out_shape=(jax.ShapeDtypeStruct((patches, 2, dl),...  61.8 us
    pallas_call x1, Pallas kernels, on_device(): pl.pallas_call(settle, out_shape=(jax.ShapeDtypeStruct(byte_out.shape, BF...  1.91 us

profile of v5, /device:TPU:1, one launch (start us, length us, event | category | flops | bytes accessed | tf_op | source)
XLA Modules:
  0.0 64.5 jit_solution(10207407750249222796)
XLA Ops:
  0.6 61.8 %shard_map.149 = (bf16[128,2,1024]{2,1,0:T(2,128)(2,1)}, bf16[32,4,512]{2,1,0:T(4,128)(2,1)}) custom-call(bf16[1024,1024]{1,0:T(8,128)(2,1)} %bitcast.6, bf16[3,1024,256]{2,1,0:T(8,128)(2,1)} %bitcast.7, bf16[256,1024]{1,0:T(8,128)(2,1)} %wo_hbm.1, bf16[1024,1024]{1,0:T(8,128)(2,1)} %up_hbm.1, bf16[1024,1024]{1,0:T(8,128)(2,1)} %down_hbm.1, ...), custom_call_target="tpu_custom_call" | custom-call | tf_op jit(solution)/shard_map/pallas_call | solution.py:712
  62.5 1.9 %shard_map.150 = (bf16[128,2,1024]{2,1,0:T(2,128)(2,1)}, bf16[128,512]{1,0:T(8,128)(2,1)}) custom-call(bf16[128,2,1024]{2,1,0:T(2,128)(2,1)} %get-tuple-element.4.a_hbm, bf16[32,4,512]{2,1,0:T(4,128)(2,1)} %get-tuple-element.5.b_hbm), custom_call_target="tpu_custom_call" | custom-call | tf_op jit(solution)/shard_map/pallas_call | solution.py:725

commit v6 on v5

--- a/solution.py
+++ b/solution.py
@@ -18,6 +18,8 @@
 ZN = 4
 CHUNKS = 4
 HD = 128
+UPWARD = (0, 3)
+DOWNWARD = (1, 2)
 
 
 def dot(a, b):
@@ -344,7 +346,7 @@
         def _():
             act_on(up_copy(y, d, yu_s, yu_r))
 
-        @pl.when((y == 0) | ((y == 1) & (d % 2 == 1)))
+        @pl.when((y == 0) | ((y == 1) & (d in DOWNWARD)))
         def _():
             act_on(down_copy(y, d, yd_s, yd_r))
 
@@ -359,29 +361,33 @@
         def _():
             up_copy(y3, d, yu_s, yu_r).wait_recv()
 
-        if d % 2 == 0:
+        if d in UPWARD:
 
             @pl.when(inner)
             def _():
                 relay_up(y3, d).start()
 
     def take_up(d):
-        @pl.when((y == last) | ((y == 0) & (d % 2 == 1)))
+        @pl.when((y == last) | ((y == 0) & (d in DOWNWARD)))
         def _():
             down_copy(y1, d, yd_s, yd_r).wait_recv()
 
-        if d % 2 == 1:
+        if d in DOWNWARD:
 
             @pl.when(outer)
             def _():
                 relay_down(y1, d).start()
 
-    def take_far():
+    def take_far_up():
         @pl.when(y >= 2)
         def _():
-            for d in (0, 2):
+            for d in UPWARD:
                 relay_up(y2, d).wait_recv()
-            for d in (1, 3):
+
+    def take_far_down():
+        @pl.when(y >= 2)
+        def _():
+            for d in DOWNWARD:
                 relay_down(y2, d).wait_recv()
 
     q_give = remote(qbuf.at[0], qbuf.at[1], c_s.at[0], c_r.at[0], sibling)
@@ -403,7 +409,7 @@
     acc[...] = jnp.zeros(acc.shape, F32)
     factor = gscale_ref[x] * (math.log2(math.e) / math.sqrt(HD))
 
-    for d in (3, 1, 2):
+    for d in (3, 2, 1):
         xk_arrival(d).wait()
         spread_piece(d, start)
     arrived(qbuf.at[0, pl.ds(0, XN - 1)], xq_r.at[0])
@@ -411,14 +417,18 @@
 
     half_q = XN * patches // 2
 
-    def attend(yb, rels, masked):
+    def attend(yb, rels, masked, picks=None):
         chains = [(rel, part_q) for rel in rels for part_q in range(2)]
 
         def raw(chain):
             rel, part_q = chain
             wide = (part_q + 1) * XN // 2 if masked else XN
             queries = qbuf[rel].reshape(XN * patches, HD)[part_q * half_q : (part_q + 1) * half_q]
-            scores = dot_t(kvbuf[yb, 0:wide, 0].reshape(wide * patches, HD), queries)
+            if picks:
+                k = jnp.concatenate([kvbuf[yb, src(d), 0] for d in picks], axis=0)
+            else:
+                k = kvbuf[yb, 0:wide, 0].reshape(wide * patches, HD)
+            scores = dot_t(k, queries)
             if masked:
                 kk = lax.broadcasted_iota(jnp.int32, scores.shape, 0)
                 qq = lax.broadcasted_iota(jnp.int32, scores.shape, 1) + part_q * half_q
@@ -444,13 +454,14 @@
             m_ref[rel, :, cut] = new
             l_ref[rel, :, cut] = l_ref[rel, :, cut] * keep + fold(jnp.sum, e)
             wide = scores.shape[0] // patches
-            vt = jnp.concatenate([kvbuf[yb, k, 1] for k in range(wide)], axis=1)
+            slots = [src(d) for d in picks] if picks else range(wide)
+            vt = jnp.concatenate([kvbuf[yb, slot, 1] for slot in slots], axis=1)
             acc[rel, :, cut] = acc[rel, :, cut] * keep + dot(vt, e.astype(BF16))
 
-    def run(yb, rels):
+    def run(yb, rels, picks=None):
         @pl.when(yb < y)
         def _():
-            attend(yb, rels, False)
+            attend(yb, rels, False, picks)
 
 
     attend(y, (0,), True)
@@ -458,22 +469,24 @@
     take_up(0)
     q_give.wait_recv()
     attend(y, (1,), True)
-    for d in (3, 1, 2):
+    for d in (3, 2, 1):
         take_up(d)
         take_down(d)
     run(y3, (1, 0))
     run(y1, (1, 0))
     arrived(bfar, bf_r.at[0])
     lax.fori_loop(0, CHUNKS, bulk_combine, 0)
-    take_far()
-    run(y2, (1,))
+    take_far_up()
+    run(y2, (1, 0), UPWARD)
+    take_far_down()
+    run(y2, (1,), DOWNWARD)
     opart[...] = (acc[1] / l_ref[1]).astype(BF16)
     stpart[...] = jnp.zeros(stpart.shape, F32)
     stpart[0:1] = m_ref[1]
     stpart[1:2] = l_ref[1]
     o_give.start()
     st_give.start()
-    run(y2, (0,))
+    run(y2, (0,), DOWNWARD)
     o_give.wait_recv()
     st_give.wait_recv()
     m0, m1 = m_ref[0], stget[0:1]
@@ -612,12 +625,12 @@
 
     @pl.when(inner)
     def _():
-        for d in (0, 2):
+        for d in UPWARD:
             relay_up(y3, d).wait_send()
 
     @pl.when(outer)
     def _():
-        for d in (1, 3):
+        for d in DOWNWARD:
             relay_down(y1, d).wait_send()
 
     for copy in (q_give, o_give, st_give):

time: 64.7 us -> 64.6 us (level)
  no operation moved by 1% of the time
where the time goes in v6:
time: 64.6 us; the launch traced here: 64.4 us
  Pallas kernels  63.6 us (98%)
  between operations  0.8 us (1%)
    pallas_call x1, Pallas kernels, on_device(): pl.pallas_call(kernel, out_shape=(jax.ShapeDtypeStruct((patches, 2, dl),...  61.7 us
    pallas_call x1, Pallas kernels, on_device(): pl.pallas_call(settle, out_shape=(jax.ShapeDtypeStruct(byte_out.shape, BF...  1.91 us

profile of v6, /device:TPU:1, one launch (start us, length us, event | category | flops | bytes accessed | tf_op | source)
XLA Modules:
  0.0 64.4 jit_solution(9317978914420202301)
XLA Ops:
  0.6 61.7 %shard_map.149 = (bf16[128,2,1024]{2,1,0:T(2,128)(2,1)}, bf16[32,4,512]{2,1,0:T(4,128)(2,1)}) custom-call(bf16[1024,1024]{1,0:T(8,128)(2,1)} %bitcast.6, bf16[3,1024,256]{2,1,0:T(8,128)(2,1)} %bitcast.7, bf16[256,1024]{1,0:T(8,128)(2,1)} %wo_hbm.1, bf16[1024,1024]{1,0:T(8,128)(2,1)} %up_hbm.1, bf16[1024,1024]{1,0:T(8,128)(2,1)} %down_hbm.1, ...), custom_call_target="tpu_custom_call" | custom-call | tf_op jit(solution)/shard_map/pallas_call | solution.py:725
  62.4 1.9 %shard_map.150 = (bf16[128,2,1024]{2,1,0:T(2,128)(2,1)}, bf16[128,512]{1,0:T(8,128)(2,1)}) custom-call(bf16[128,2,1024]{2,1,0:T(2,128)(2,1)} %get-tuple-element.4.a_hbm, bf16[32,4,512]{2,1,0:T(4,128)(2,1)} %get-tuple-element.5.b_hbm), custom_call_target="tpu_custom_call" | custom-call | tf_op jit(solution)/shard_map/pallas_call | solution.py:738

commit v7 on v6

--- a/solution.py
+++ b/solution.py
@@ -275,13 +275,6 @@
                 arrived(pin.at[h, CHUNKS - 1], an_r.at[CHUNKS - 1])
             else:
                 arrived(pin.at[h], ag_r.at[d - 1])
-        if d == 2:
-            for c in range(CHUNKS):
-                for copy in bulk_far(c):
-                    copy.start()
-            for c in range(CHUNKS):
-                bulk_up(c, 1).start()
-                bulk_down(c, 0).start()
         at = pl.ds(pl.multiple_of(h * piece, piece), piece)
         v = pin[h].reshape(patches, piece).astype(F32)
         square = square + jnp.sum(v * v, axis=-1, keepdims=True)
@@ -404,6 +397,12 @@
     for d in (2, 1, 3):
         xq_copy(d).start()
     qbuf[0, x] = qkvs[x, 0]
+    for c in range(CHUNKS):
+        for copy in bulk_far(c):
+            copy.start()
+    for c in range(CHUNKS):
+        bulk_up(c, 1).start()
+        bulk_down(c, 0).start()
     m_ref[...] = jnp.full(m_ref.shape, NEG, F32)
     l_ref[...] = jnp.zeros(l_ref.shape, F32)
     acc[...] = jnp.zeros(acc.shape, F32)

time: 64.6 us -> 64.5 us (level)
  no operation moved by 1% of the time
where the time goes in v7:
time: 64.5 us; the launch traced here: 64.4 us
  Pallas kernels  63.6 us (99%)
  between operations  0.8 us (1%)
    pallas_call x1, Pallas kernels, on_device(): pl.pallas_call(kernel, out_shape=(jax.ShapeDtypeStruct((patches, 2, dl),...  61.6 us
    pallas_call x1, Pallas kernels, on_device(): pl.pallas_call(settle, out_shape=(jax.ShapeDtypeStruct(byte_out.shape, BF...  1.91 us

profile of v7, /device:TPU:1, one launch (start us, length us, event | category | flops | bytes accessed | tf_op | source)
XLA Modules:
  0.0 64.4 jit_solution(10534271962511007924)
XLA Ops:
  0.6 61.6 %shard_map.149 = (bf16[128,2,1024]{2,1,0:T(2,128)(2,1)}, bf16[32,4,512]{2,1,0:T(4,128)(2,1)}) custom-call(bf16[1024,1024]{1,0:T(8,128)(2,1)} %bitcast.6, bf16[3,1024,256]{2,1,0:T(8,128)(2,1)} %bitcast.7, bf16[256,1024]{1,0:T(8,128)(2,1)} %wo_hbm.1, bf16[1024,1024]{1,0:T(8,128)(2,1)} %up_hbm.1, bf16[1024,1024]{1,0:T(8,128)(2,1)} %down_hbm.1, ...), custom_call_target="tpu_custom_call" | custom-call | tf_op jit(solution)/shard_map/pallas_call | solution.py:724
  62.3 1.9 %shard_map.150 = (bf16[128,2,1024]{2,1,0:T(2,128)(2,1)}, bf16[128,512]{1,0:T(8,128)(2,1)}) custom-call(bf16[128,2,1024]{2,1,0:T(2,128)(2,1)} %get-tuple-element.4.a_hbm, bf16[32,4,512]{2,1,0:T(4,128)(2,1)} %get-tuple-element.5.b_hbm), custom_call_target="tpu_custom_call" | custom-call | tf_op jit(solution)/shard_map/pallas_call | solution.py:737
